TPU v7x, 32 devices: a whole 2x2x4 slice. The times are simulated.
32 devices in a mesh: dp: 4 (over y, x), ep: 8 (over z, core).
Axes of the slice: x: 2, y: 2, z: 4, core: 2. Of those that a mesh axis runs over, the one named last changes fastest.
Arguments:
- attn_heads: bfloat16 [8, 256, 2048], P('ep', None, 'dp'), may hold values from -6 to 6
- residual: bfloat16 [8, 256, 2048], P('ep', 'dp'), may hold values from -6 to 6
- w_out: bfloat16 [2048, 2048], P('dp'), may hold values from -0.125 to 0.125
- gain_post: bfloat16 [2048], replicated, may hold values from 0.5 to 1.5
- w_router: bfloat16 [2048, 60], replicated, may hold values from -0.125 to 0.125
- expert_ids: int32 [8, 256, 4], P('ep', 'dp'), may hold values from 0 to 59, all different within a row; in each aligned block of 64 rows (0 to 63, 64 to 127, ..., all dimensions but the last counted through in order) at most 8 rows name the same one
- expert_slot: int32 [60], replicated, may hold values from 0 to 63, as said below
- w_gate: bfloat16 [64, 2048, 1408], P('ep', None, 'dp'), may hold values from -0.125 to 0.125
- w_up: bfloat16 [64, 2048, 1408], P('ep', None, 'dp'), may hold values from -0.125 to 0.125
- w_down: bfloat16 [64, 1408, 2048], P('ep', 'dp'), may hold values from -0.15625 to 0.15625
- w_shared_gate: bfloat16 [2048, 5632], P(None, 'ep'), may hold values from -0.125 to 0.125
- w_shared_up: bfloat16 [2048, 5632], P(None, 'ep'), may hold values from -0.125 to 0.125
- w_shared_down: bfloat16 [5632, 2048], P('ep'), may hold values from -0.078125 to 0.078125
- w_shared_score: bfloat16 [2048], replicated, may hold values from -0.125 to 0.125
- gain_final: bfloat16 [2048], replicated, may hold values from 0.5 to 1.5
Outputs:
- mixed_out: bfloat16 [8, 256, 2048], P('ep', 'dp')
- final_out: bfloat16 [8, 256, 2048], P('ep', 'dp')
Inputs may be any that keep to these rules, and one draw needn't show every extreme that they name: `expert_ids`: each row names 4 different experts. Within the 64 rows of one device no expert is named by more than 8 rows, and in some device one expert is named by exactly 8 rows. All entries differ; expert e uses entry expert_slot[e] of w_gate, w_up and w_down, and index i of ep holds positions i * 8 to (i + 1) * 8 - 1.
All inputs are finite; a program needn't handle non-finite values.
Results may differ from a plain program's by a relative error of at most 0.02.
Values may be sent and summed in bfloat16 or wider, within the bound.
A program may use at most 128 MiB of HBM per device.

v0:
```python
import jax
import jax.numpy as jnp
from jax import lax
from jax.sharding import PartitionSpec as P

MOST = 8


eps_norm = 1e-06


def rms_scale(values_in, gain_vec):
    values = values_in.astype(jnp.float32)
    return (
        values
        * lax.rsqrt(jnp.mean(values * values, axis=-1, keepdims=True) + eps_norm)
        * gain_vec.astype(jnp.float32)
    )


def expert_partial(rows_in, w_gate, w_up, w_down):
    gate_part = jnp.einsum("semd,edf->semf", rows_in, w_gate, preferred_element_type=jnp.float32)
    up_part = jnp.einsum("semd,edf->semf", rows_in, w_up, preferred_element_type=jnp.float32)
    hidden = (jax.nn.silu(gate_part) * up_part).astype(jnp.bfloat16)
    return jnp.einsum("semf,efd->semd", hidden, w_down, preferred_element_type=jnp.float32)


def per_device(
    attn_heads,
    residual,
    w_out,
    gain_post,
    w_router,
    expert_ids,
    expert_slot,
    w_gate,
    w_up,
    w_down,
    w_shared_gate,
    w_shared_up,
    w_shared_down,
    w_shared_score,
    gain_final,
):
    local_heads = attn_heads[0]
    model_width = residual.shape[2]
    row_block = local_heads
    projected = lax.psum_scatter(
        jnp.dot(row_block, w_out, preferred_element_type=jnp.float32).astype(jnp.bfloat16),
        "dp",
        scatter_dimension=0,
        tiled=True,
    ).astype(jnp.float32)
    hidden_state = (residual[0].astype(jnp.float32) + projected).astype(jnp.bfloat16)
    normed = rms_scale(hidden_state, gain_post).astype(jnp.bfloat16)
    logits = jnp.dot(normed, w_router, preferred_element_type=jnp.float32)
    chosen = expert_ids[0]
    expert_count = w_router.shape[1]
    one_hot = chosen[:, :, None] == jnp.arange(expert_count, dtype=jnp.int32)[None, None, :]
    picked = jnp.sum(jnp.where(one_hot, logits[:, None, :], 0.0), axis=2)
    exp_logits = jnp.exp(picked)
    route_weights = (exp_logits / jnp.sum(exp_logits, axis=1, keepdims=True)).astype(jnp.bfloat16)
    experts_here = w_gate.shape[0]
    groups = lax.axis_size("ep")
    positions = experts_here * groups
    buffer_cells = positions * MOST
    expert_hits = jnp.any(one_hot, axis=1).astype(jnp.int32)
    earlier = jnp.cumsum(expert_hits, axis=0) - expert_hits
    slot_rank = jnp.sum(jnp.where(one_hot, earlier[:, None, :], 0), axis=2)
    position = jnp.sum(jnp.where(one_hot, expert_slot[None, None, :], 0), axis=2)
    buffer_index = position * MOST + slot_rank
    placed = buffer_index[:, :, None] == jnp.arange(buffer_cells, dtype=jnp.int32)[None, None, :]
    dispatch_mat = jnp.any(placed, axis=1).astype(jnp.bfloat16)
    combine_mat = jnp.sum(
        jnp.where(placed, route_weights.astype(jnp.float32)[:, :, None], 0.0), axis=1
    ).astype(jnp.bfloat16)
    outgoing = jnp.einsum(
        "rc,rd->cd", dispatch_mat, normed, preferred_element_type=jnp.float32
    ).astype(jnp.bfloat16)
    outgoing = outgoing.reshape(groups, experts_here, MOST, model_width)
    dp_count = lax.axis_size("dp")
    copies = jnp.broadcast_to(outgoing[None], (dp_count,) + outgoing.shape).reshape(
        (dp_count * groups, experts_here, MOST, model_width)
    )
    partial_value = expert_partial(
        lax.all_to_all(copies, ("dp", "ep"), split_axis=0, concat_axis=0, tiled=True),
        w_gate,
        w_up,
        w_down,
    ).astype(jnp.bfloat16)
    returned_all = lax.all_to_all(
        partial_value, ("dp", "ep"), split_axis=0, concat_axis=0, tiled=True
    )
    returned = jnp.sum(
        returned_all.reshape(dp_count, groups, experts_here, MOST, model_width).astype(jnp.float32),
        axis=0,
    ).astype(jnp.bfloat16)
    routed = jnp.dot(
        combine_mat, returned.reshape(buffer_cells, model_width), preferred_element_type=jnp.float32
    )
    row_block = lax.all_gather(normed, "ep", axis=0, tiled=True)
    gate_part = jnp.dot(row_block, w_shared_gate, preferred_element_type=jnp.float32)
    up_part = jnp.dot(row_block, w_shared_up, preferred_element_type=jnp.float32)
    hidden_all = (jax.nn.silu(gate_part) * up_part).astype(jnp.bfloat16)
    row_block = hidden_all
    shared_sum = lax.psum_scatter(
        jnp.dot(row_block, w_shared_down, preferred_element_type=jnp.float32).astype(jnp.bfloat16),
        "ep",
        scatter_dimension=0,
        tiled=True,
    ).astype(jnp.float32)
    shared_score = jax.nn.sigmoid(
        jnp.dot(normed, w_shared_score, preferred_element_type=jnp.float32)
    )
    mixed_out = (
        hidden_state.astype(jnp.float32) + shared_score[:, None] * shared_sum + routed
    ).astype(jnp.bfloat16)
    final_out = rms_scale(mixed_out, gain_final).astype(jnp.bfloat16)
    return (mixed_out[None], final_out[None])


def solution(mesh):
    in_specs = (
        P("ep", None, "dp"),
        P("ep", "dp", None),
        P("dp", None),
        P(),
        P(),
        P("ep", "dp", None),
        P(),
        P("ep", None, "dp"),
        P("ep", None, "dp"),
        P("ep", "dp", None),
        P(None, "ep"),
        P(None, "ep"),
        P("ep", None),
        P(),
        P(),
    )
    out_specs = (P("ep", "dp", None), P("ep", "dp", None))
    return jax.shard_map(
        per_device, mesh=mesh, in_specs=in_specs, out_specs=out_specs, check_vma=False
    )
```

profile of v0, /device:TPU:0, one launch (start us, length us, event | category | flops | bytes accessed | tf_op | source)
XLA Modules:
  0.0 522.7 jit_solution(2066058382093305351)
XLA Ops:
  7.3 3.5 convolution_convert_fusion.2
  11.3 0.1 select_reduce_fusion.3
  11.6 29.8 %reduce-scatter.3.cloned.1.call-done = bf16[64,2048]{1,0:T(8,128)(2,1)} async-done(((bf16[256,2048]{1,0:T(8,128)(2,1)}), bf16[64,2048]{1,0:T(8,128)(2,1)}) %reduce-scatter.3.cloned.1.call-update) | async-done | bytes 262160 | tf_op jit(solution)/shard_map/reduce_scatter | solution.py:48
  41.4 1.1 fusion.27
  42.5 1.1 fusion.29
  43.6 0.8 convolution_convert_fusion
  44.4 1.1 broadcast_in_dim.80
  45.5 189.4 %all_to_all.10 = bf16[32,8,8,2048]{3,2,1,0:T(8,128)(2,1)} all-to-all(bf16[32,8,8,2048]{3,2,1,0:T(8,128)(2,1)S(1)} %bitcast.88), channel_id=1, replica_groups=mesh['dp'=4,'ep'=8] {'dp','ep'}, dimensions={0} | all-to-all | bytes 16777216 | tf_op jit(solution)/shard_map/all_to_all | solution.py:86
  234.9 14.1 %fusion.4 = f32[8,32,8,352]{3,2,1,0:T(8,128)} fusion(bf16[8,2048,352]{1,2,0:T(8,128)(2,1)} %param.22, bf16[32,8,8,2048]{3,2,1,0:T(8,128)(2,1)} %all_to_all.10), kind=kOutput, calls=%fused_computation.4 | convolution fusion | flops 2952790016 | bytes 22806528 | tf_op jit(solution)/shard_map/semd,edf->semf/dot_general | solution.py:22
  249.0 23.5 %convert_bitcast_fusion = bf16[32,8,8,2048]{3,2,0,1:T(8,128)(2,1)} fusion(bf16[8,352,2048]{2,1,0:T(8,128)(2,1)} %param.24, f32[8,32,8,352]{3,2,1,0:T(8,128)} %fusion.4, bf16[8,2048,352]{1,2,0:T(8,128)(2,1)} %param.23, bf16[32,8,8,2048]{3,2,1,0:T(8,128)(2,1)} %all_to_all.10), kind=kOutput, calls=%fused_computation.6 | convolution fusion | flops 5914099712 | bytes 42729472 | tf_op jit(solution)/shard_map/semf,efd->semd/dot_general | solution.py:25
  272.5 8.3 %copy.34 = bf16[32,8,8,2048]{3,2,1,0:T(8,128)(2,1)} copy(bf16[32,8,8,2048]{3,2,0,1:T(8,128)(2,1)} %convert_bitcast_fusion) | data formatting | bytes 16777216 | tf_op jit(solution)/shard_map/convert_element_type | solution.py:90
  280.7 3.7 all-to-all-start.1
  284.5 0.7 all-gather.2.cloned.1.call-update
  285.2 0.2 reduce-scatter.5.cloned.1.call-start
  285.4 52.7 %all-gather.2.cloned.1.call-done = bf16[512,2048]{1,0:T(8,128)(2,1)} async-done(((bf16[64,2048]{1,0:T(8,128)(2,1)}), bf16[512,2048]{1,0:T(8,128)(2,1)}) %all-gather.2.cloned.1.call-update) | async-done | bytes 2097168 | tf_op jit(solution)/shard_map/all_gather | solution.py:101
  338.1 5.2 %fusion.43 = f32[512,704]{0,1:T(8,128)} fusion(bf16[512,2048]{1,0:T(8,128)(2,1)} %all-gather.2.cloned.1.call-done, bf16[2048,704]{0,1:T(8,128)(2,1)} %param.25), kind=kOutput, calls=%fused_computation.61 | convolution fusion | flops 1476395008 | bytes 6422528 | tf_op jit(solution)/shard_map/dot_general | solution.py:102
  343.3 7.7 %convolution_convert_fusion.1 = bf16[512,2048]{1,0:T(8,128)(2,1)} fusion(bf16[704,2048]{1,0:T(8,128)(2,1)S(1)} %copy-done, bf16[512,2048]{1,0:T(8,128)(2,1)} %all-gather.2.cloned.1.call-done, bf16[2048,704]{0,1:T(8,128)(2,1)} %param.26, f32[512,704]{0,1:T(8,128)} %fusion.43), kind=kOutput, calls=%fused_computation.17 | convolution fusion | flops 2956001280 | bytes 11403264 | tf_op jit(solution)/shard_map/dot_general | solution.py:107
  351.1 1.2 fusion.44
  352.4 0.1 select_reduce_fusion
  352.6 0.2 fusion.23
  352.7 153.1 %all-to-all-done.1 = bf16[32,8,8,2048]{3,2,1,0:T(8,128)(2,1)} async-done(((bf16[32,8,8,2048]{3,2,1,0:T(8,128)(2,1)}), bf16[32,8,8,2048]{3,2,1,0:T(8,128)(2,1)}, u32[]{:S(2)}, u32[]{:S(2)}) %all-to-all-start.1) | async-done | bytes 8388640 | tf_op jit(solution)/shard_map/all_to_all | solution.py:91
  505.8 7.3 %reduce_sum.81 = bf16[8,8,8,2048]{3,2,1,0:T(8,128)(2,1)} reduce(bf16[4,8,8,8,2048]{4,3,2,1,0:T(8,128)(2,1)} %bitcast.15, bf16[]{:T(256)} %constant.24.clone.1), dimensions={0}, to_apply=%region_11.12 | reduce | flops 3145728 | bytes 10485762 | tf_op jit(solution)/shard_map/reduce_sum | solution.py:94
  513.1 2.2 fusion.24
  515.4 0.8 fusion.32
  (43 shorter events, 0.9 us)
Async XLA Ops:
  7.2 336.2 %copy-start = (bf16[704,2048]{1,0:T(8,128)(2,1)S(1)}, bf16[704,2048]{1,0:T(8,128)(2,1)}, u32[]{:S(2)}) copy-start(bf16[704,2048]{1,0:T(8,128)(2,1)} %param.27) | copy-start | bytes 8650756
  7.2 3.6 copy-start.6
  7.2 4.1 copy-start.7
  7.2 4.1 copy-start.10
  7.2 34.2 %copy-start.3 = (bf16[1,64,2048]{2,1,0:T(8,128)(2,1)S(1)}, bf16[1,64,2048]{2,1,0:T(8,128)(2,1)}, u32[]{:S(2)}) copy-start(bf16[1,64,2048]{2,1,0:T(8,128)(2,1)} %param.16) | copy-start | bytes 786436
  7.2 34.2 %reduce-scatter.3.cloned.1.call-start = ((), (), s32[]{:S(2)}) async-start(), calls=%async_computation.4 | async-start | bytes 1310720 | tf_op jit(solution)/shard_map/reduce_scatter | solution.py:48
  43.6 1.9 copy-start.1
  280.7 225.1 %all-to-all-start.1 = ((bf16[32,8,8,2048]{3,2,1,0:T(8,128)(2,1)}), bf16[32,8,8,2048]{3,2,1,0:T(8,128)(2,1)}, u32[]{:S(2)}, u32[]{:S(2)}) async-start(bf16[32,8,8,2048]{3,2,1,0:T(8,128)(2,1)} %copy.34), calls=%async_computation.3 | async-start | bytes 16777216 | tf_op jit(solution)/shard_map/all_to_all | solution.py:91
  284.4 53.7 %all-gather.2.cloned.1.call-start = ((), (), s32[]{:S(2)}) async-start(), calls=%async_computation.5 | async-start | bytes 2359296 | tf_op jit(solution)/shard_map/all_gather | solution.py:101
  285.2 227.9 %reduce-scatter.5.cloned.1.call-start = ((), (), s32[]{:S(2)}) async-start(), calls=%async_computation.6 | async-start | bytes 2359296 | tf_op jit(solution)/shard_map/reduce_scatter | solution.py:106
  343.3 7.7 %copy-start.8 = (bf16[2048]{0:T(1024)(128)(2,1)S(1)}, bf16[2048]{0:T(1024)(128)(2,1)}, u32[]{:S(2)}) copy-start(bf16[2048]{0:T(1024)(128)(2,1)} %param.28) | copy-start | bytes 12292
  343.3 7.8 %copy-start.9 = (bf16[2048]{0:T(1024)(128)(2,1)S(1)}, bf16[2048]{0:T(1024)(128)(2,1)}, u32[]{:S(2)}) copy-start(bf16[2048]{0:T(1024)(128)(2,1)} %param.29) | copy-start | bytes 12292
  343.3 7.8 %copy-start.2 = (bf16[64,2048]{1,0:T(8,128)(2,1)S(1)}, bf16[64,2048]{1,0:T(8,128)(2,1)}, u32[]{:S(2)}) copy-start(bf16[64,2048]{1,0:T(8,128)(2,1)} %copy-done.1) | copy-start | bytes 786436
  505.8 7.3 %copy-start.4 = (bf16[64,2048]{1,0:T(8,128)(2,1)S(1)}, bf16[64,2048]{1,0:T(8,128)(2,1)}, u32[]{:S(2)}) copy-start(bf16[64,2048]{1,0:T(8,128)(2,1)} %reduce-scatter.3.cloned.1.call-done) | copy-start | bytes 786436
  515.3 0.9 copy-start.5
Sparse Core Ops, SparseCore 0:
  10.9 30.4 reduce-scatter.2
  287.5 50.5 all-gather.1
  351.2 73.7 reduce-scatter.4
where the time goes:
time: 523 us
  waiting for transfers between devices  236 us (45%)
  blocking collectives  189 us (36%)
  matrix products  58.4 us (11%)
  between operations  14 us (3%)
  other arithmetic  11.1 us (2%)
  local copies, waits for them, and re-layouts  9.59 us (2%)
    all_to_all x1, blocking collectives, per_device(): lax.all_to_all(copies, ('dp', 'ep'), split_axis=0, concat_axis=0, tiled=T...  189 us
    all_to_all x1, waiting for transfers between devices, per_device(): lax.all_to_all(partial_value, ('dp', 'ep'), split_axis=0, concat_axis=0,...  153 us
    all_gather x1, waiting for transfers between devices, per_device(): row_block = lax.all_gather(normed, 'ep', axis=0, tiled=True)  52.7 us
    reduce_scatter x1, waiting for transfers between devices, per_device(): lax.psum_scatter(jnp.dot(row_block, w_out, preferred_element_type=jnp.flo...  29.8 us
    dot_general x1, matrix products, expert_partial(): jnp.einsum('semf,efd->semd', hidden, w_down, preferred_element_type=jnp.f...  23.5 us
    dot_general x1, matrix products, expert_partial(): jnp.einsum('semd,edf->semf', rows_in, w_gate, preferred_element_type=jnp....  14.1 us
  transfers between devices with their start and end apart: 4, of which 3 were waited for; matrix products, arithmetic and copies ran while one was open for 4% of the time, Pallas kernels for 0%

commit v1 on v0

v1 whole, which is shorter than its diff:
```python
import functools

import jax
import jax.numpy as jnp
from jax import lax
from jax.experimental import pallas as pl
from jax.experimental.pallas import tpu as pltpu
from jax.sharding import PartitionSpec as P

MOST = 8
N_DP = 4

eps_norm = 1e-06

f32 = jnp.float32
bf16 = jnp.bfloat16


def place(axes=("dp", "ep")):
    dp = lax.axis_index("dp")
    ep = lax.axis_index("ep")
    core = ep % 2
    z = ep // 2
    low = dp % 2
    high = dp // 2
    flip_low = 1 - 2 * low
    flip_high = 2 - 4 * high
    first = dp + (1 - core) * flip_low + core * flip_high
    second = dp + core * flip_low + (1 - core) * flip_high
    return dp, z, core, first, second, 3 - dp


def greet(z_count, dp, z, core):
    barrier = pltpu.get_barrier_semaphore()

    def hello(d, e):
        pl.semaphore_signal(barrier, inc=1, device_id={"dp": d, "ep": e})

    for k in range(1, N_DP):
        hello((dp + k) % N_DP, z * 2 + core)
    for k in range(1, z_count):
        hello(dp, ((z + k) % z_count) * 2 + core)
    hello(dp, z * 2 + 1 - core)
    pl.semaphore_wait(barrier, N_DP - 1 + z_count - 1 + 1)


def gather_kernel(
    z_count, tok, attn, w_out, residual, gain, rows, hidden,
    outbox, inbox, own,
    ps, pr, zs, zr, fs, fr, ss, sr, cs, cr, local,
):
    dp, z, core, first, second, far = place()
    greet(z_count, dp, z, core)

    def send(src, dst, s_sem, r_sem, d, e):
        return pltpu.make_async_remote_copy(
            src_ref=src, dst_ref=dst, send_sem=s_sem, recv_sem=r_sem,
            device_id={"dp": d, "ep": e},
        )

    me = z * 2 + core
    pending = []
    projections = []
    for k in (2, 1, 3):
        q = (dp + k) % N_DP
        outbox[k - 1] = jnp.dot(
            attn[pl.ds(pl.multiple_of(q * tok, tok), tok), :], w_out[...],
            preferred_element_type=f32,
        ).astype(bf16)
        copy = send(outbox.at[k - 1], inbox.at[k - 1], ps.at[k - 1], pr.at[k - 1], q, me)
        copy.start()
        projections.append((k, copy))
    total = residual[...].astype(f32) + jnp.dot(
        attn[pl.ds(pl.multiple_of(dp * tok, tok), tok), :], w_out[...],
        preferred_element_type=f32,
    )
    for k, copy in projections:
        copy.wait_recv()
        total = total + inbox[k - 1].astype(f32)
    state = total.astype(bf16)
    hidden[...] = state
    wide = state.astype(f32)
    own[...] = (
        wide * lax.rsqrt(jnp.mean(wide * wide, axis=-1, keepdims=True) + eps_norm)
        * gain[...].astype(f32)
    ).astype(bf16)
    for k, copy in projections:
        copy.wait_send()

    def block(k, c, d):
        return rows.at[(((z + z_count - k) % z_count) * 2 + c) * N_DP + d]

    keep = pltpu.make_async_copy(own, block(0, core, dp), local.at[0])
    keep.start()

    def over_first(k):
        src = own if k == 0 else block(k, core, dp)
        return send(src, block(k, core, dp), fs.at[k], fr.at[k], first, me)

    def over_second(k, j):
        d = dp if j == 0 else first
        src = own if k == 0 and j == 0 else block(k, core, d)
        return send(src, block(k, core, d), ss.at[2 * k + j], sr.at[2 * k + j], second, me)

    def over_core(k, j):
        d = (dp, first, second, far)[j]
        src = own if k == 0 and j == 0 else block(k, core, d)
        return send(src, block(k, core, d), cs.at[4 * k + j], cr.at[4 * k + j], dp, z * 2 + 1 - core)

    def arrived(sem, ref):
        pltpu.make_async_copy(ref, ref, sem).wait()

    def go(copy):
        copy.start()
        pending.append(copy)

    go(over_first(0))
    go(over_second(0, 0))
    for k in range(1, z_count):
        go(send(own, block(0, core, dp), zs.at[k], zr.at[k], dp, ((z + k) % z_count) * 2 + core))
    go(over_core(0, 0))

    def tail(k):
        for j, d in ((0, second), (1, far)):
            arrived(sr.at[2 * k + j], block(k, core, d))
            go(over_core(k, 2 + j))

    for k in range(z_count):
        if k > 0:
            arrived(zr.at[k], block(k, core, dp))
            go(over_first(k))
            go(over_second(k, 0))
            go(over_core(k, 0))
        arrived(fr.at[k], block(k, core, first))
        go(over_second(k, 1))
        go(over_core(k, 1))
        if k > 0:
            tail(k - 1)
    tail(z_count - 1)
    for k in range(z_count):
        for j, d in ((0, dp), (1, second), (2, first), (3, far)):
            arrived(cr.at[4 * k + j], block(k, 1 - core, d))
    for copy in pending:
        copy.wait_send()
    keep.wait()


def project_and_gather(z_count, attn, w_out, residual, gain):
    tok, width = residual.shape
    count = z_count * 2 * N_DP
    dma = pltpu.SemaphoreType.DMA
    vmem = pl.BlockSpec(memory_space=pltpu.VMEM)
    return pl.pallas_call(
        functools.partial(gather_kernel, z_count, tok),
        out_shape=(
            jax.ShapeDtypeStruct((count, tok, width), bf16),
            jax.ShapeDtypeStruct((tok, width), bf16),
        ),
        in_specs=[vmem] * 4,
        out_specs=(pl.BlockSpec(memory_space=pl.ANY), vmem),
        scratch_shapes=[
            pltpu.VMEM((N_DP - 1, tok, width), bf16),
            pltpu.VMEM((N_DP - 1, tok, width), bf16),
            pltpu.VMEM((tok, width), bf16),
            dma((N_DP - 1,)), dma((N_DP - 1,)),
            dma((z_count,)), dma((z_count,)),
            dma((z_count,)), dma((z_count,)),
            dma((2 * z_count,)), dma((2 * z_count,)),
            dma((4 * z_count,)), dma((4 * z_count,)),
            dma((1,)),
        ],
        compiler_params=pltpu.CompilerParams(
            collective_id=0, has_side_effects=True, vmem_limit_bytes=32 << 20
        ),
        name="project_gather",
    )(attn, w_out, residual, gain)


def scatter_kernel(
    z_count, part, hidden, gain, mixed, final,
    acc, from_core, from_second, from_first, from_z,
    cs, cr, ss, sr, fs, fr, zs, zr, local,
):
    dp, z, core, first, second, far = place()
    greet(z_count, dp, z, core)
    me = z * 2 + core
    dest = (dp, first, second, far)
    pending = []
    order = list(range(1, z_count)) + [0]

    def send(src, dst, s_sem, r_sem, d, e):
        copy = pltpu.make_async_remote_copy(
            src_ref=src, dst_ref=dst, send_sem=s_sem, recv_sem=r_sem,
            device_id={"dp": d, "ep": e},
        )
        copy.start()
        pending.append(copy)

    def level(k):
        return (z + z_count - k) % z_count

    def arrived(sem, ref):
        pltpu.make_async_copy(ref, ref, sem).wait()

    def begin(k, j):
        i = 4 * k + j
        there = (dp, second, first, far)[j]
        pltpu.make_async_copy(
            part.at[(level(k) * 2 + core) * N_DP + dest[j]], acc.at[i], local.at[i]
        ).start()
        send(
            part.at[(level(k) * 2 + 1 - core) * N_DP + there], from_core.at[i],
            cs.at[i], cr.at[i], dp, z * 2 + 1 - core,
        )

    for j in (3, 2, 1, 0):
        for k in order:
            begin(k, j)

    def pair(k, j):
        i = 4 * k + j
        arrived(local.at[i], acc.at[i])
        arrived(cr.at[i], from_core.at[i])
        return acc[i].astype(f32) + from_core[i].astype(f32)

    for j in (3, 2):
        for k in order:
            acc[4 * k + j] = pair(k, j).astype(bf16)
            i = 2 * k + j - 2
            send(acc.at[4 * k + j], from_second.at[i], ss.at[i], sr.at[i], second, me)

    def summed(k, j):
        i = 2 * k + j
        value = pair(k, j)
        arrived(sr.at[i], from_second.at[i])
        return value + from_second[i].astype(f32)

    def pass_first(k):
        acc[4 * k + 1] = summed(k, 1).astype(bf16)
        send(acc.at[4 * k + 1], from_first.at[k], fs.at[k], fr.at[k], first, me)

    def pass_z(k):
        value = summed(k, 0)
        arrived(fr.at[k], from_first.at[k])
        value = value + from_first[k].astype(f32)
        if k > 0:
            acc[4 * k] = value.astype(bf16)
            send(acc.at[4 * k], from_z.at[k], zs.at[k], zr.at[k], dp, level(k) * 2 + core)
            return None
        return value

    for k in order:
        pass_first(k)
    for k in order:
        value = pass_z(k)
    for k in range(1, z_count):
        arrived(zr.at[k], from_z.at[k])
        value = value + from_z[k].astype(f32)
    out = (hidden[...].astype(f32) + value).astype(bf16)
    mixed[...] = out
    wide = out.astype(f32)
    final[...] = (
        wide * lax.rsqrt(jnp.mean(wide * wide, axis=-1, keepdims=True) + eps_norm)
        * gain[...].astype(f32)
    ).astype(bf16)
    for copy in pending:
        copy.wait_send()


def reduce_and_norm(z_count, part, hidden, gain):
    tok, width = hidden.shape
    dma = pltpu.SemaphoreType.DMA
    vmem = pl.BlockSpec(memory_space=pltpu.VMEM)
    shape = jax.ShapeDtypeStruct((tok, width), bf16)
    boxes = [4 * z_count, 4 * z_count, 2 * z_count, z_count, z_count]
    sems = [4 * z_count] * 2 + [2 * z_count] * 2 + [z_count] * 4 + [4 * z_count]
    return pl.pallas_call(
        functools.partial(scatter_kernel, z_count),
        out_shape=(shape, shape),
        in_specs=[pl.BlockSpec(memory_space=pl.ANY), vmem, vmem],
        out_specs=(vmem, vmem),
        scratch_shapes=[pltpu.VMEM((n, tok, width), bf16) for n in boxes]
        + [dma((n,)) for n in sems],
        compiler_params=pltpu.CompilerParams(
            collective_id=1, has_side_effects=True, vmem_limit_bytes=56 << 20
        ),
        name="reduce_norm",
    )(part, hidden, gain)


def expert_kernel(
    groups, experts, tok, where_ref, x_ref, send_ref, gate_ref, up_ref, down_ref, back_ref, shared_ref,
    out_ref, cells, results,
):
    step = pl.program_id(0)
    wide = N_DP * MOST

    @pl.when(step < groups)
    def _():
        picked = jnp.dot(send_ref[0], x_ref[0], preferred_element_type=f32).astype(bf16)
        for e in range(experts):
            cells[e, pl.ds(pl.multiple_of(step * wide, wide), wide), :] = picked[e * wide:(e + 1) * wide]

    @pl.when((step >= groups) & (step < groups + experts))
    def _():
        e = step - groups
        rows = cells[e]
        gate = jnp.dot(rows, gate_ref[0], preferred_element_type=f32)
        up = jnp.dot(rows, up_ref[0], preferred_element_type=f32)
        hidden = (gate / (1.0 + jnp.exp(-gate)) * up).astype(bf16)
        result = jnp.dot(hidden, down_ref[0], preferred_element_type=f32).astype(bf16)
        for g in range(groups):
            results[g, pl.ds(pl.multiple_of(e * wide, wide), wide), :] = result[g * wide:(g + 1) * wide]

    @pl.when(step >= groups + experts)
    def _():
        g = step - groups - experts
        out_ref[0] = jnp.dot(back_ref[0], results[g], preferred_element_type=f32).astype(bf16)
        mine = pl.ds(pl.multiple_of(where_ref[0] * tok, tok), tok)
        out_ref[0, mine, :] = (out_ref[0, mine, :].astype(f32) + shared_ref[0].astype(f32)).astype(bf16)


def run_experts(x, send_mat, back_mat, w_gate, w_up, w_down, shared):
    groups, rows, width = x.shape
    experts, _, units = w_gate.shape
    cells = send_mat.shape[1]
    tok = rows // N_DP
    per_expert = groups * N_DP * MOST

    def at_group(i, *_):
        return (jnp.minimum(i, groups - 1), 0, 0)

    def at_expert(i, *_):
        return (jnp.clip(i - groups, 0, experts - 1), 0, 0)

    def at_end(i, *_):
        return (jnp.clip(i - groups - experts, 0, groups - 1), 0, 0)

    return pl.pallas_call(
        functools.partial(expert_kernel, groups, experts, tok),
        out_shape=jax.ShapeDtypeStruct((groups, rows, width), bf16),
        grid_spec=pltpu.PrefetchScalarGridSpec(
            num_scalar_prefetch=1,
            grid=(2 * groups + experts,),
            in_specs=[
                pl.BlockSpec((1, rows, width), at_group),
                pl.BlockSpec((1, cells, rows), at_group),
                pl.BlockSpec((1, width, units), at_expert),
                pl.BlockSpec((1, width, units), at_expert),
                pl.BlockSpec((1, units, width), at_expert),
                pl.BlockSpec((1, rows, cells), at_end),
                pl.BlockSpec((1, tok, width), at_end),
            ],
            out_specs=pl.BlockSpec((1, rows, width), at_end),
            scratch_shapes=[
                pltpu.VMEM((experts, per_expert, width), bf16),
                pltpu.VMEM((groups, cells, width), bf16),
            ],
        ),
        compiler_params=pltpu.CompilerParams(vmem_limit_bytes=56 << 20),
        name="experts",
    )(lax.axis_index("dp").astype(jnp.int32).reshape(1), x, send_mat, w_gate, w_up, w_down, back_mat, shared)


def per_device(
    attn_heads,
    residual,
    w_out,
    gain_post,
    w_router,
    expert_ids,
    expert_slot,
    w_gate,
    w_up,
    w_down,
    w_shared_gate,
    w_shared_up,
    w_shared_down,
    w_shared_score,
    gain_final,
):
    groups = lax.axis_size("ep")
    z_count = groups // 2
    experts_here = w_gate.shape[0]
    expert_count = w_router.shape[1]
    width = residual.shape[2]
    tok = residual.shape[1]
    rows = N_DP * tok
    spread = N_DP * MOST

    ids = lax.all_gather(expert_ids[0], ("ep", "dp"), axis=0, tiled=False)
    ids = ids.reshape(groups * N_DP, tok, -1)
    names = ids[..., None] == jnp.arange(expert_count, dtype=jnp.int32)
    chosen = jnp.any(names, axis=2)
    here = lax.axis_index("ep") * experts_here + jnp.arange(experts_here, dtype=jnp.int32)
    local = (expert_slot[:, None] == here[None, :]).astype(f32)
    hits = jnp.einsum("stx,xe->ste", chosen.astype(bf16), local.astype(bf16), preferred_element_type=f32)
    below = jnp.tril(jnp.ones((tok, tok), bf16), -1)
    rank = jnp.einsum("ut,ste->sue", below, hits.astype(bf16), preferred_element_type=f32)
    part = (jnp.arange(groups * N_DP, dtype=jnp.int32) % N_DP * MOST)[:, None, None]
    cell = jnp.where(hits > 0.5, rank.astype(jnp.int32) + part, -1).reshape(groups, rows, experts_here)
    numbers = jnp.arange(spread, dtype=jnp.int32)
    send_mat = (jnp.swapaxes(cell, 1, 2)[:, :, None, :] == numbers[None, None, :, None]).astype(bf16)
    send_mat = send_mat.reshape(groups, experts_here * spread, rows)

    x_all, hidden_state = project_and_gather(
        z_count, attn_heads[0], w_out, residual[0], gain_post.reshape(1, width)
    )
    x = x_all.reshape(groups, rows, width)

    logits = jnp.einsum("grd,dx->grx", x, w_router, preferred_element_type=f32)
    powers = jnp.where(chosen.reshape(groups, rows, expert_count), jnp.exp(logits), 0.0)
    weights = powers / jnp.sum(powers, axis=-1, keepdims=True)
    mine = jnp.einsum("grx,xe->gre", weights.astype(bf16), local.astype(bf16), preferred_element_type=f32)
    back_mat = jnp.where(cell[:, :, :, None] == numbers, mine[:, :, :, None], 0.0)
    back_mat = back_mat.astype(bf16).reshape(groups, rows, experts_here * spread)

    line = lax.dynamic_index_in_dim(
        x.reshape(groups, N_DP, tok, width), lax.axis_index("dp"), axis=1, keepdims=False
    ).reshape(groups * tok, width)
    gate_part = jnp.dot(line, w_shared_gate, preferred_element_type=f32)
    up_part = jnp.dot(line, w_shared_up, preferred_element_type=f32)
    shared_hidden = (jax.nn.silu(gate_part) * up_part).astype(bf16)
    score = jax.nn.sigmoid(jnp.dot(line, w_shared_score, preferred_element_type=f32))
    shared = (
        jnp.dot(shared_hidden, w_shared_down, preferred_element_type=f32) * score[:, None]
    ).astype(bf16).reshape(groups, tok, width)

    partial_sums = run_experts(x, send_mat, back_mat, w_gate, w_up, w_down, shared)
    mixed_out, final_out = reduce_and_norm(
        z_count, partial_sums.reshape(groups * N_DP, tok, width), hidden_state,
        gain_final.reshape(1, width),
    )
    return (mixed_out[None], final_out[None])


def solution(mesh):
    in_specs = (
        P("ep", None, "dp"),
        P("ep", "dp", None),
        P("dp", None),
        P(),
        P(),
        P("ep", "dp", None),
        P(),
        P("ep", None, "dp"),
        P("ep", None, "dp"),
        P("ep", "dp", None),
        P(None, "ep"),
        P(None, "ep"),
        P("ep", None),
        P(),
        P(),
    )
    out_specs = (P("ep", "dp", None), P("ep", "dp", None))
    return jax.shard_map(
        per_device, mesh=mesh, in_specs=in_specs, out_specs=out_specs, check_vma=False
    )
```

time: 523 us -> 297 us (0.57)
  waiting for transfers between devices: 236 us -> 0 us
  Pallas kernels: 0 us -> 148 us
  blocking collectives: 189 us -> 72.4 us
  local copies, waits for them, and re-layouts: 9.59 us -> 51.9 us
  matrix products: 58.4 us -> 17.9 us
  between operations: 14 us -> 0.81 us
  other arithmetic: 11.1 us -> 4.34 us
    all_to_all x1 -> x0, blocking collectives: 189 us -> none  [per_device(): lax.all_to_all(copies, ('dp', 'ep'), split_axis=0, concat_axis=0, tiled=T...]
    all_to_all x1 -> x0, waiting for transfers between devices: 153 us -> none  [per_device(): lax.all_to_all(partial_value, ('dp', 'ep'), split_axis=0, concat_axis=0,...]
    pallas_call x0 -> x3, Pallas kernels: none -> 148 us  [the longest x1 59.5 us: project_and_gather(): pl.pallas_call(functools.partial(gather_kernel, z_count, tok), out_shape=...]
    all_gather x0 -> x1, blocking collectives: none -> 72.4 us  [per_device(): ids = lax.all_gather(expert_ids[0], ('ep', 'dp'), axis=0, tiled=False)]
    all_gather x1 -> x0, waiting for transfers between devices: 52.7 us -> none  [per_device(): row_block = lax.all_gather(normed, 'ep', axis=0, tiled=True)]
    unnamed x23 -> x33, local copies, waits for them, and re-layouts: 0.06 us -> 42.8 us
    dot_general x9 -> x7, matrix products: 58.4 us -> 17.9 us  [the longest x1 7.69 us: per_device(): jnp.dot(shared_hidden, w_shared_down, preferred_element_type=f32)]
    reduce_scatter x2 -> x0, waiting for transfers between devices: 29.8 us -> none  [the longest x1 29.8 us: per_device(): lax.psum_scatter(jnp.dot(row_block, w_out, preferred_element_type=jnp.flo...]
  transfers between devices with their start and end apart: 4 -> 0, of which waited for: 3 -> 0; matrix products, arithmetic and copies ran while one was open for 4% -> 0% of each run, Pallas kernels for 0% -> 0%
where the time goes in v1:
time: 297 us; the launch traced here: 295 us
  Pallas kernels  148 us (50%)
  blocking collectives  72.4 us (24%)
  local copies, waits for them, and re-layouts  51.9 us (17%)
  matrix products  17.9 us (6%)
  other arithmetic  4.34 us (1%)
    all_gather x1, blocking collectives, per_device(): ids = lax.all_gather(expert_ids[0], ('ep', 'dp'), axis=0, tiled=False)  72.4 us
    pallas_call x1, Pallas kernels, project_and_gather(): pl.pallas_call(functools.partial(gather_kernel, z_count, tok), out_shape=...  59.5 us
    pallas_call x1, Pallas kernels, reduce_and_norm(): pl.pallas_call(functools.partial(scatter_kernel, z_count), out_shape=(sha...  53.3 us
    unnamed x33, local copies, waits for them, and re-layouts  42.8 us
    pallas_call x1, Pallas kernels, run_experts(): pl.pallas_call(functools.partial(expert_kernel, groups, experts, tok), ou...  34.8 us
    dot_general x1, matrix products, per_device(): jnp.dot(shared_hidden, w_shared_down, preferred_element_type=f32)  7.69 us
    dot_general x1, matrix products, per_device(): logits = jnp.einsum('grd,dx->grx', x, w_router, preferred_element_type=f32)  6.05 us

profile of v1, /device:TPU:0, one launch (start us, length us, event | category | flops | bytes accessed | tf_op | source)
XLA Modules:
  0.0 295.0 jit_solution(12670957280875014198)
XLA Ops:
  0.7 0.8 reshape.61.gain
  1.5 1.6 copy-done.3
  3.1 0.9 copy-done.4
  4.1 0.9 copy-done.5
  5.0 59.5 %project_gather.1 = (bf16[32,64,2048]{2,1,0:T(8,128)(2,1)S(1)}, bf16[64,2048]{1,0:T(8,128)(2,1)S(1)}) custom-call(bf16[256,512]{1,0:T(8,128)(2,1)S(1)} %bitcast.48, bf16[512,2048]{1,0:T(8,128)(2,1)S(1)} %copy-done.3, bf16[64,2048]{1,0:T(8,128)(2,1)S(1)} %bitcast.49, bf16[1,2048]{1,0:T(2,128)(2,1)S(1)} %reshape.61.gain), custom_call_target="tpu_custom_call" | custom-call | tf_op jit(solution)/shard_map/project_gather/pallas_call | solution.py:153
  64.6 0.7 copy-done.6
  65.4 3.8 %copy-done.12 = bf16[2048,704]{0,1:T(8,128)(2,1)S(1)} copy-done((bf16[2048,704]{0,1:T(8,128)(2,1)S(1)}, bf16[2048,704]{0,1:T(8,128)(2,1)}, u32[]{:S(2)}) %copy-start.12) | copy-done | bytes 2883608
  69.2 2.8 fusion.31
  72.0 0.6 fusion.32
  72.7 7.7 %multiply_convert_fusion = bf16[512,2048]{1,0:T(8,128)(2,1)} fusion(bf16[704,2048]{1,0:T(8,128)(2,1)S(1)} %copy-done, f32[512]{0:T(512)S(1)} %add_divide_fusion, bf16[512,2048]{1,0:T(8,128)(2,1)} %bitcast.53, bf16[2048,704]{0,1:T(8,128)(2,1)} %param.26, f32[512,704]{0,1:T(8,128)} %fusion.31), kind=kOutput, calls=%fused_computation | convolution fusion | flops 2957049856 | bytes 11405312 | tf_op jit(solution)/shard_map/dot_general | solution.py:426
  80.4 72.4 %all_gather.3 = s32[32,64,4]{1,2,0:T(4,128)S(1)} all-gather(s32[1,64,4]{1,2,0:T(4,128)S(1)} %copy-done.11), channel_id=1, replica_groups=mesh['dp'=4,'ep'=8] {'ep','dp'}, dimensions={0}, use_global_device_ids=true | all-gather | bytes 33792 | tf_op jit(solution)/shard_map/all_gather | solution.py:391
  154.2 1.5 eq.80
  155.7 2.0 copy.55
  158.1 6.1 %fusion.3 = f32[8,256,60]{1,2,0:T(8,128)S(1)} fusion(bf16[8,256,2048]{2,1,0:T(8,128)(2,1)} %bitcast.46, pred[8,256,60]{1,0,2:T(8,128)(4,1)S(1)} %reshape.64, bf16[2048,60]{0,1:T(8,128)(2,1)S(1)} %copy-done.8), kind=kOutput, calls=%fused_computation.9 | convolution fusion | flops 503439360 | bytes 9248768 | tf_op jit(solution)/shard_map/grd,dx->grx/dot_general | solution.py:411
  164.3 1.1 broadcast_in_dim.50
  165.4 2.2 copy.57
  167.8 2.4 select_convert_fusion.back_ref
  170.2 1.2 fusion.1.send_ref
  171.4 16.2 %copy.58.gate_ref = bf16[8,2048,352]{2,1,0:T(8,128)(2,1)} copy(bf16[8,2048,352]{1,2,0:T(8,128)(2,1)} %param.22) | data formatting | bytes 23068672 | tf_op args[7]
  187.6 15.3 %copy.59.up_ref = bf16[8,2048,352]{2,1,0:T(8,128)(2,1)} copy(bf16[8,2048,352]{1,2,0:T(8,128)(2,1)} %param.23) | data formatting | bytes 23068672 | tf_op args[8]
  202.9 34.8 %experts.1 = bf16[8,256,2048]{2,1,0:T(8,128)(2,1)} custom-call(s32[1]{0:T(128)} %bitcast.where_ref, bf16[8,256,2048]{2,1,0:T(8,128)(2,1)} %bitcast.47, bf16[8,256,256]{2,1,0:T(8,128)(2,1)} %fusion.1.send_ref, bf16[8,2048,352]{2,1,0:T(8,128)(2,1)} %copy.58.gate_ref, bf16[8,2048,352]{2,1,0:T(8,128)(2,1)} %copy.59.up_ref, bf16[8,352,2048]{2,1,0:T(8,128)(2,1)} %down_ref.1, ...), custom_call_target="tpu_custom_call" | custom-call | tf_op jit(solution)/shard_map/experts/pallas_call | solution.py:339
  238.3 53.3 %reduce_norm.1 = (bf16[64,2048]{1,0:T(8,128)(2,1)}, bf16[64,2048]{1,0:T(8,128)(2,1)}) custom-call(bf16[32,64,2048]{2,1,0:T(8,128)(2,1)} %bitcast.50, bf16[64,2048]{1,0:T(8,128)(2,1)} %copy-done.6, bf16[1,2048]{1,0:T(2,128)(2,1)} %reshape.68.gain), custom_call_target="tpu_custom_call" | custom-call | tf_op jit(solution)/shard_map/reduce_norm/pallas_call | solution.py:277
  291.6 1.7 copy.74
  293.3 1.7 copy.75
  (43 shorter events, 2.9 us)
Async XLA Ops:
  0.6 72.1 %copy-start = (bf16[704,2048]{1,0:T(8,128)(2,1)S(1)}, bf16[704,2048]{1,0:T(8,128)(2,1)}, u32[]{:S(2)}) copy-start(bf16[704,2048]{1,0:T(8,128)(2,1)} %param.27) | copy-start | bytes 8650756
  1.5 1.6 copy-start.3
  3.1 0.9 copy-start.4
  4.1 0.9 copy-start.5
  64.5 0.7 copy-start.6
  65.3 6.7 %copy-start.2 = (bf16[32,64,2048]{2,1,0:T(8,128)(2,1)}, bf16[32,64,2048]{2,1,0:T(8,128)(2,1)S(1)}, u32[]{:S(2)}) copy-start(bf16[32,64,2048]{2,1,0:T(8,128)(2,1)S(1)} %get-tuple-element.6) | copy-start | bytes 25165828
  65.3 3.9 %copy-start.12 = (bf16[2048,704]{0,1:T(8,128)(2,1)S(1)}, bf16[2048,704]{0,1:T(8,128)(2,1)}, u32[]{:S(2)}) copy-start(bf16[2048,704]{0,1:T(8,128)(2,1)} %param.25) | copy-start | bytes 8650756
  65.4 6.6 %copy-start.7 = (bf16[8,1,64,2048]{3,2,1,0:T(8,128)(2,1)}, bf16[8,1,64,2048]{3,2,1,0:T(8,128)(2,1)S(1)}, u32[]{:S(2)}) copy-start(bf16[8,1,64,2048]{3,2,1,0:T(8,128)(2,1)S(1)} %constant_dynamic-slice_fusion) | copy-start | bytes 6291460
  69.2 2.8 copy-start.9
  72.7 7.7 %copy-start.11 = (s32[1,64,4]{1,2,0:T(4,128)S(1)}, s32[1,64,4]{1,2,0:T(4,128)}, u32[]{:S(2)}) copy-start(s32[1,64,4]{1,2,0:T(4,128)} %param.20) | copy-start | bytes 3076
  72.7 80.7 %copy-start.13 = (s32[60]{0:T(128)S(1)}, s32[60]{0:T(128)}, u32[]{:S(2)}) copy-start(s32[60]{0:T(128)} %param.21) | copy-start | bytes 724
  155.7 2.4 copy-start.8
  202.9 34.8 %copy-start.10 = (bf16[2048]{0:T(1024)(128)(2,1)S(1)}, bf16[2048]{0:T(1024)(128)(2,1)}, u32[]{:S(2)}) copy-start(bf16[2048]{0:T(1024)(128)(2,1)} %param.29) | copy-start | bytes 12292
  238.3 56.7 %copy-start.1 = (bf16[704,2048]{1,0:T(8,128)(2,1)S(1)}, bf16[704,2048]{1,0:T(8,128)(2,1)}, u32[]{:S(2)}) copy-start(bf16[704,2048]{1,0:T(8,128)(2,1)} %param.27) | copy-start | bytes 8650756

commit v2 on v1

--- a/solution.py
+++ b/solution.py
@@ -2,6 +2,7 @@
 
 import jax
 import jax.numpy as jnp
+import numpy as np
 from jax import lax
 from jax.experimental import pallas as pl
 from jax.experimental.pallas import tpu as pltpu
@@ -44,10 +45,16 @@
     pl.semaphore_wait(barrier, N_DP - 1 + z_count - 1 + 1)
 
 
+def rows_dot(a, b):
+    return lax.dot_general(a, b, (((1,), (1,)), ((), ())), preferred_element_type=f32)
+
+
 def gather_kernel(
-    z_count, tok, attn, w_out, residual, gain, rows, hidden,
-    outbox, inbox, own,
-    ps, pr, zs, zr, fs, fr, ss, sr, cs, cr, local,
+    z_count, tok, attn, w_out, residual, gain, ids, gate_hbm, up_hbm, down_hbm,
+    rows, hidden, ids_out, shared,
+    outbox, inbox, own, names, gate_w, up_w, down_w, line,
+    ps, pr, zs, zr, fs, fr, ss, sr, cs, cr, local, weight_sem, line_sem,
+    izs, izr, ifs, ifr, iss, isr, ics, icr,
 ):
     dp, z, core, first, second, far = place()
     greet(z_count, dp, z, core)
@@ -61,7 +68,43 @@
     me = z * 2 + core
     pending = []
     projections = []
-    for k in (2, 1, 3):
+    loads = [
+        pltpu.make_async_copy(src, dst, weight_sem.at[i])
+        for i, (src, dst) in enumerate(((gate_hbm, gate_w), (up_hbm, up_w), (down_hbm, down_w)))
+    ]
+    for load in loads:
+        load.start()
+
+    def arrived(sem, ref):
+        pltpu.make_async_copy(ref, ref, sem).wait()
+
+    def go(copy):
+        copy.start()
+        pending.append(copy)
+
+    names[core, dp, z] = ids[...]
+    for k in range(1, z_count):
+        spot = names.at[core, dp, z]
+        go(send(spot, spot, izs.at[k], izr.at[k], dp, ((z + k) % z_count) * 2 + core))
+
+    def names_step(step):
+        if step == 0:
+            for k in range(1, z_count):
+                arrived(izr.at[k], names.at[core, dp, (z + z_count - k) % z_count])
+            spot = names.at[core, dp]
+            go(send(spot, spot, ifs.at[0], ifr.at[0], first, me))
+        elif step == 1:
+            arrived(ifr.at[0], names.at[core, first])
+            for i, d in ((0, dp), (1, first)):
+                spot = names.at[core, d]
+                go(send(spot, spot, iss.at[i], isr.at[i], second, me))
+        elif step == 2:
+            arrived(isr.at[0], names.at[core, second])
+            arrived(isr.at[1], names.at[core, far])
+            spot = names.at[core]
+            go(send(spot, spot, ics.at[0], icr.at[0], dp, z * 2 + 1 - core))
+
+    for step, k in enumerate((2, 1, 3)):
         q = (dp + k) % N_DP
         outbox[k - 1] = jnp.dot(
             attn[pl.ds(pl.multiple_of(q * tok, tok), tok), :], w_out[...],
@@ -70,6 +113,7 @@
         copy = send(outbox.at[k - 1], inbox.at[k - 1], ps.at[k - 1], pr.at[k - 1], q, me)
         copy.start()
         projections.append((k, copy))
+        names_step(step)
     total = residual[...].astype(f32) + jnp.dot(
         attn[pl.ds(pl.multiple_of(dp * tok, tok), tok), :], w_out[...],
         preferred_element_type=f32,
@@ -107,12 +151,30 @@
         src = own if k == 0 and j == 0 else block(k, core, d)
         return send(src, block(k, core, d), cs.at[4 * k + j], cr.at[4 * k + j], dp, z * 2 + 1 - core)
 
-    def arrived(sem, ref):
-        pltpu.make_async_copy(ref, ref, sem).wait()
-
-    def go(copy):
-        copy.start()
-        pending.append(copy)
+    def share(c):
+        for start in range(0, z_count, 4):
+            some = range(start, min(start + 4, z_count))
+            moves = []
+            for i, k in enumerate(some):
+                if c == 1:
+                    arrived(cr.at[4 * k], block(k, 1 - core, dp))
+                elif k == 0:
+                    keep.wait()
+                where = block(k, core if c == 0 else 1 - core, dp)
+                move = pltpu.make_async_copy(where, line.at[pl.ds(i * tok, tok)], line_sem.at[i])
+                move.start()
+                moves.append(move)
+            for move in moves:
+                move.wait()
+            count = len(moves) * tok
+            x = line[:count]
+            gate = rows_dot(x, gate_w[...])
+            up = rows_dot(x, up_w[...])
+            units = (gate / (1.0 + jnp.exp(-gate)) * up).astype(bf16)
+            out = jnp.dot(units, down_w[...], preferred_element_type=f32).astype(bf16)
+            for i, k in enumerate(some):
+                level = (z + z_count - k) % z_count
+                shared[level * 2 + (core if c == 0 else 1 - core)] = out[i * tok:(i + 1) * tok]
 
     go(over_first(0))
     go(over_second(0, 0))
@@ -134,18 +196,28 @@
         arrived(fr.at[k], block(k, core, first))
         go(over_second(k, 1))
         go(over_core(k, 1))
+        if k == z_count - 1:
+            for load in loads:
+                load.wait()
+            share(0)
         if k > 0:
             tail(k - 1)
+    share(1)
     tail(z_count - 1)
+    arrived(icr.at[0], names.at[1 - core])
+    for c in range(2):
+        for d in range(N_DP):
+            for level in range(z_count):
+                ids_out[level * 2 + c, :, d * tok:(d + 1) * tok] = names[c, d, level][:, :tok]
     for k in range(z_count):
-        for j, d in ((0, dp), (1, second), (2, first), (3, far)):
+        for j, d in ((1, second), (2, first), (3, far)):
             arrived(cr.at[4 * k + j], block(k, 1 - core, d))
     for copy in pending:
         copy.wait_send()
-    keep.wait()
-
-
-def project_and_gather(z_count, attn, w_out, residual, gain):
+
+
+def project_and_gather(z_count, attn, w_out, residual, gain, ids, gate, up, down):
+    units = down.shape[0]
     tok, width = residual.shape
     count = z_count * 2 * N_DP
     dma = pltpu.SemaphoreType.DMA
@@ -155,25 +227,36 @@
         out_shape=(
             jax.ShapeDtypeStruct((count, tok, width), bf16),
             jax.ShapeDtypeStruct((tok, width), bf16),
+            jax.ShapeDtypeStruct((z_count * 2, 8, N_DP * tok), jnp.int32),
+            jax.ShapeDtypeStruct((z_count * 2, tok, width), bf16),
         ),
-        in_specs=[vmem] * 4,
-        out_specs=(pl.BlockSpec(memory_space=pl.ANY), vmem),
+        in_specs=[vmem] * 5 + [pl.BlockSpec(memory_space=pl.ANY)] * 3,
+        out_specs=(pl.BlockSpec(memory_space=pl.ANY), vmem, vmem, vmem),
         scratch_shapes=[
             pltpu.VMEM((N_DP - 1, tok, width), bf16),
             pltpu.VMEM((N_DP - 1, tok, width), bf16),
             pltpu.VMEM((tok, width), bf16),
+            pltpu.VMEM((2, N_DP, z_count, 8, 128), jnp.int32),
+            pltpu.VMEM((units, width), bf16),
+            pltpu.VMEM((units, width), bf16),
+            pltpu.VMEM((units, width), bf16),
+            pltpu.VMEM((4 * tok, width), bf16),
             dma((N_DP - 1,)), dma((N_DP - 1,)),
             dma((z_count,)), dma((z_count,)),
             dma((z_count,)), dma((z_count,)),
             dma((2 * z_count,)), dma((2 * z_count,)),
             dma((4 * z_count,)), dma((4 * z_count,)),
-            dma((1,)),
+            dma((1,)), dma((3,)), dma((4,)),
+            dma((z_count,)), dma((z_count,)),
+            dma((1,)), dma((1,)),
+            dma((2,)), dma((2,)),
+            dma((1,)), dma((1,)),
         ],
         compiler_params=pltpu.CompilerParams(
-            collective_id=0, has_side_effects=True, vmem_limit_bytes=32 << 20
+            collective_id=0, has_side_effects=True, vmem_limit_bytes=48 << 20
         ),
         name="project_gather",
-    )(attn, w_out, residual, gain)
+    )(attn, w_out, residual, gain, ids, gate, up, down)
 
 
 def scatter_kernel(
@@ -289,15 +372,36 @@
 
 
 def expert_kernel(
-    groups, experts, tok, where_ref, x_ref, send_ref, gate_ref, up_ref, down_ref, back_ref, shared_ref,
-    out_ref, cells, results,
+    groups, experts, tok, where_ref, x_ref, ids_ref, router_ref, cell_expert_ref, cell_number_ref,
+    before_ref, source_ref, gate_ref, up_ref, down_ref, shared_ref,
+    out_ref, cells, results, back, logits_ref,
 ):
     step = pl.program_id(0)
     wide = N_DP * MOST
 
     @pl.when(step < groups)
     def _():
-        picked = jnp.dot(send_ref[0], x_ref[0], preferred_element_type=f32).astype(bf16)
+        x = x_ref[0]
+        logits = rows_dot(x, router_ref[...])
+        logits_ref[step] = logits
+        lined = logits.T
+        numbers = lax.broadcasted_iota(jnp.int32, lined.shape, 0)
+        chosen = numbers == ids_ref[0, 0:1, :]
+        for k in range(1, 4):
+            chosen = chosen | (numbers == ids_ref[0, k:k + 1, :])
+        powers = jnp.where(chosen, jnp.exp(lined), 0.0)
+        weights = (powers / jnp.sum(powers, axis=0, keepdims=True)).astype(bf16)
+        hit = jnp.where(chosen, 1.0, 0.0).astype(bf16)
+        rank = jnp.dot(hit, before_ref[...], preferred_element_type=f32) + source_ref[...]
+        at_cell = cell_expert_ref[...]
+        named = jnp.dot(at_cell, hit, preferred_element_type=f32)
+        spot = jnp.dot(at_cell, rank.astype(bf16), preferred_element_type=f32)
+        weight = jnp.dot(at_cell, weights, preferred_element_type=f32)
+        here = (named > 0.5) & (spot == cell_number_ref[...])
+        back[step] = jnp.where(here, weight, 0.0).T.astype(bf16)
+        picked = jnp.dot(
+            jnp.where(here, 1.0, 0.0).astype(bf16), x, preferred_element_type=f32
+        ).astype(bf16)
         for e in range(experts):
             cells[e, pl.ds(pl.multiple_of(step * wide, wide), wide), :] = picked[e * wide:(e + 1) * wide]
 
@@ -305,8 +409,8 @@
     def _():
         e = step - groups
         rows = cells[e]
-        gate = jnp.dot(rows, gate_ref[0], preferred_element_type=f32)
-        up = jnp.dot(rows, up_ref[0], preferred_element_type=f32)
+        gate = rows_dot(rows, gate_ref[0])
+        up = rows_dot(rows, up_ref[0])
         hidden = (gate / (1.0 + jnp.exp(-gate)) * up).astype(bf16)
         result = jnp.dot(hidden, down_ref[0], preferred_element_type=f32).astype(bf16)
         for g in range(groups):
@@ -315,17 +419,31 @@
     @pl.when(step >= groups + experts)
     def _():
         g = step - groups - experts
-        out_ref[0] = jnp.dot(back_ref[0], results[g], preferred_element_type=f32).astype(bf16)
+        out_ref[0] = jnp.dot(back[g], results[g], preferred_element_type=f32).astype(bf16)
         mine = pl.ds(pl.multiple_of(where_ref[0] * tok, tok), tok)
-        out_ref[0, mine, :] = (out_ref[0, mine, :].astype(f32) + shared_ref[0].astype(f32)).astype(bf16)
-
-
-def run_experts(x, send_mat, back_mat, w_gate, w_up, w_down, shared):
+        last = where_ref[1]
+        columns = logits_ref[g, mine, :]
+        lane = lax.broadcasted_iota(jnp.int32, columns.shape, 1)
+        score = jnp.sum(jnp.where(lane == last, columns, 0.0), axis=1, keepdims=True)
+        score = 1.0 / (1.0 + jnp.exp(-score))
+        out_ref[0, mine, :] = (
+            out_ref[0, mine, :].astype(f32) + score * shared_ref[0].astype(f32)
+        ).astype(bf16)
+
+
+def run_experts(x, ids, router, cell_expert, score_row, w_gate, w_up, w_down, shared):
     groups, rows, width = x.shape
-    experts, _, units = w_gate.shape
-    cells = send_mat.shape[1]
+    experts, units, _ = w_gate.shape
+    cells, known = cell_expert.shape
     tok = rows // N_DP
-    per_expert = groups * N_DP * MOST
+    spread = N_DP * MOST
+    place_of = np.arange(rows)
+    before = (place_of[:, None] < place_of[None, :]) & (
+        place_of[:, None] // tok == place_of[None, :] // tok
+    )
+    before = jnp.asarray(before, bf16)
+    source = jnp.asarray(place_of[None, :] // tok * MOST, f32)
+    cell_number = jnp.asarray(np.arange(cells)[:, None] % spread, f32)
 
     def at_group(i, *_):
         return (jnp.minimum(i, groups - 1), 0, 0)
@@ -336,6 +454,10 @@
     def at_end(i, *_):
         return (jnp.clip(i - groups - experts, 0, groups - 1), 0, 0)
 
+    def whole(i, *_):
+        return (0, 0)
+
+    where = jnp.stack([lax.axis_index("dp").astype(jnp.int32), jnp.int32(score_row)])
     return pl.pallas_call(
         functools.partial(expert_kernel, groups, experts, tok),
         out_shape=jax.ShapeDtypeStruct((groups, rows, width), bf16),
@@ -344,22 +466,28 @@
             grid=(2 * groups + experts,),
             in_specs=[
                 pl.BlockSpec((1, rows, width), at_group),
-                pl.BlockSpec((1, cells, rows), at_group),
-                pl.BlockSpec((1, width, units), at_expert),
-                pl.BlockSpec((1, width, units), at_expert),
+                pl.BlockSpec((1, 8, rows), at_group),
+                pl.BlockSpec(router.shape, whole),
+                pl.BlockSpec((cells, known), whole),
+                pl.BlockSpec((cells, 1), whole),
+                pl.BlockSpec((rows, rows), whole),
+                pl.BlockSpec((1, rows), whole),
                 pl.BlockSpec((1, units, width), at_expert),
-                pl.BlockSpec((1, rows, cells), at_end),
+                pl.BlockSpec((1, units, width), at_expert),
+                pl.BlockSpec((1, units, width), at_expert),
                 pl.BlockSpec((1, tok, width), at_end),
             ],
             out_specs=pl.BlockSpec((1, rows, width), at_end),
             scratch_shapes=[
-                pltpu.VMEM((experts, per_expert, width), bf16),
+                pltpu.VMEM((experts, groups * spread, width), bf16),
                 pltpu.VMEM((groups, cells, width), bf16),
+                pltpu.VMEM((groups, rows, cells), bf16),
+                pltpu.VMEM((groups, rows, known), f32),
             ],
         ),
         compiler_params=pltpu.CompilerParams(vmem_limit_bytes=56 << 20),
         name="experts",
-    )(lax.axis_index("dp").astype(jnp.int32).reshape(1), x, send_mat, w_gate, w_up, w_down, back_mat, shared)
+    )(where, x, ids, router, cell_expert, cell_number, before, source, w_gate, w_up, w_down, shared)
 
 
 def per_device(
@@ -387,46 +515,24 @@
     tok = residual.shape[1]
     rows = N_DP * tok
     spread = N_DP * MOST
-
-    ids = lax.all_gather(expert_ids[0], ("ep", "dp"), axis=0, tiled=False)
-    ids = ids.reshape(groups * N_DP, tok, -1)
-    names = ids[..., None] == jnp.arange(expert_count, dtype=jnp.int32)
-    chosen = jnp.any(names, axis=2)
-    here = lax.axis_index("ep") * experts_here + jnp.arange(experts_here, dtype=jnp.int32)
-    local = (expert_slot[:, None] == here[None, :]).astype(f32)
-    hits = jnp.einsum("stx,xe->ste", chosen.astype(bf16), local.astype(bf16), preferred_element_type=f32)
-    below = jnp.tril(jnp.ones((tok, tok), bf16), -1)
-    rank = jnp.einsum("ut,ste->sue", below, hits.astype(bf16), preferred_element_type=f32)
-    part = (jnp.arange(groups * N_DP, dtype=jnp.int32) % N_DP * MOST)[:, None, None]
-    cell = jnp.where(hits > 0.5, rank.astype(jnp.int32) + part, -1).reshape(groups, rows, experts_here)
-    numbers = jnp.arange(spread, dtype=jnp.int32)
-    send_mat = (jnp.swapaxes(cell, 1, 2)[:, :, None, :] == numbers[None, None, :, None]).astype(bf16)
-    send_mat = send_mat.reshape(groups, experts_here * spread, rows)
-
-    x_all, hidden_state = project_and_gather(
-        z_count, attn_heads[0], w_out, residual[0], gain_post.reshape(1, width)
-    )
-    x = x_all.reshape(groups, rows, width)
-
-    logits = jnp.einsum("grd,dx->grx", x, w_router, preferred_element_type=f32)
-    powers = jnp.where(chosen.reshape(groups, rows, expert_count), jnp.exp(logits), 0.0)
-    weights = powers / jnp.sum(powers, axis=-1, keepdims=True)
-    mine = jnp.einsum("grx,xe->gre", weights.astype(bf16), local.astype(bf16), preferred_element_type=f32)
-    back_mat = jnp.where(cell[:, :, :, None] == numbers, mine[:, :, :, None], 0.0)
-    back_mat = back_mat.astype(bf16).reshape(groups, rows, experts_here * spread)
-
-    line = lax.dynamic_index_in_dim(
-        x.reshape(groups, N_DP, tok, width), lax.axis_index("dp"), axis=1, keepdims=False
-    ).reshape(groups * tok, width)
-    gate_part = jnp.dot(line, w_shared_gate, preferred_element_type=f32)
-    up_part = jnp.dot(line, w_shared_up, preferred_element_type=f32)
-    shared_hidden = (jax.nn.silu(gate_part) * up_part).astype(bf16)
-    score = jax.nn.sigmoid(jnp.dot(line, w_shared_score, preferred_element_type=f32))
-    shared = (
-        jnp.dot(shared_hidden, w_shared_down, preferred_element_type=f32) * score[:, None]
-    ).astype(bf16).reshape(groups, tok, width)
-
-    partial_sums = run_experts(x, send_mat, back_mat, w_gate, w_up, w_down, shared)
+    known = -(-(expert_count + 1) // 64) * 64
+
+    ids = jnp.swapaxes(expert_ids[0], 0, 1)
+    ids = jnp.pad(ids, ((0, 8 - ids.shape[0]), (0, 128 - tok)))
+    router = jnp.concatenate([w_router.T, w_shared_score[None, :]], axis=0)
+    router = jnp.pad(router, ((0, known - expert_count - 1), (0, 0)))
+    here = lax.axis_index("ep") * experts_here + jnp.arange(experts_here * spread, dtype=jnp.int32) // spread
+    slots = jnp.pad(expert_slot, (0, known - expert_count), constant_values=-1)
+    cell_expert = (here[:, None] == slots[None, :]).astype(bf16)
+
+    x_all, hidden_state, ids_all, shared = project_and_gather(
+        z_count, attn_heads[0], w_out, residual[0], gain_post.reshape(1, width), ids,
+        w_shared_gate.T, w_shared_up.T, w_shared_down,
+    )
+    partial_sums = run_experts(
+        x_all.reshape(groups, rows, width), ids_all, router, cell_expert, expert_count,
+        jnp.swapaxes(w_gate, 1, 2), jnp.swapaxes(w_up, 1, 2), w_down, shared,
+    )
     mixed_out, final_out = reduce_and_norm(
         z_count, partial_sums.reshape(groups * N_DP, tok, width), hidden_state,
         gain_final.reshape(1, width),

time: 297 us -> 185 us (0.62)
  blocking collectives: 72.4 us -> 0 us
  local copies, waits for them, and re-layouts: 51.9 us -> 11.5 us
  Pallas kernels: 148 us -> 171 us
  matrix products: 17.9 us -> 0 us
    all_gather x1 -> x0, blocking collectives: 72.4 us -> none  [per_device(): ids = lax.all_gather(expert_ids[0], ('ep', 'dp'), axis=0, tiled=False)]
    unnamed x33 -> x22, local copies, waits for them, and re-layouts: 42.8 us -> 9.48 us
    dot_general x7 -> x0, matrix products: 17.9 us -> none  [the longest x1 7.69 us: per_device(): jnp.dot(shared_hidden, w_shared_down, preferred_element_type=f32)]
    pallas_call x1, Pallas kernels: 53.3 us -> 63.4 us  [reduce_and_norm(): pl.pallas_call(functools.partial(scatter_kernel, z_count), out_shape=(sha...]
    pallas_call x1, Pallas kernels: 59.5 us -> 67.3 us  [project_and_gather(): pl.pallas_call(functools.partial(gather_kernel, z_count, tok), out_shape=...]
    pallas_call x1, Pallas kernels: 34.8 us -> 39.7 us  [run_experts(): pl.pallas_call(functools.partial(expert_kernel, groups, experts, tok), ou...]
    eq x4 -> x0, local copies, waits for them, and re-layouts: 3.55 us -> none  [the longest x2 3.46 us: per_device(): cell[:, :, :, None] == numbers]
    broadcast_in_dim x2 -> x1, local copies, waits for them, and re-layouts: 3.33 us -> 0.01 us  [per_device(): router = jnp.concatenate([w_router.T, w_shared_score[None, :]], axis=0)]
where the time goes in v2:
time: 185 us
  Pallas kernels  171 us (92%)
  local copies, waits for them, and re-layouts  11.5 us (6%)
  other arithmetic  2.04 us (1%)
    pallas_call x1, Pallas kernels, project_and_gather(): pl.pallas_call(functools.partial(gather_kernel, z_count, tok), out_shape=...  67.3 us
    pallas_call x1, Pallas kernels, reduce_and_norm(): pl.pallas_call(functools.partial(scatter_kernel, z_count), out_shape=(sha...  63.4 us
    pallas_call x1, Pallas kernels, run_experts(): pl.pallas_call(functools.partial(expert_kernel, groups, experts, tok), ou...  39.7 us
    unnamed x22, local copies, waits for them, and re-layouts  9.48 us

profile of v2, /device:TPU:0, one launch (start us, length us, event | category | flops | bytes accessed | tf_op | source)
XLA Modules:
  0.0 184.8 jit_solution(11379463462008512187)
XLA Ops:
  0.6 0.0 copy-start.9
  0.6 0.0 copy-start.7
  0.7 0.7 reshape.31.gain
  1.4 0.7 pad.12.ids
  2.0 1.6 copy-done.1
  3.6 0.9 copy-done.2
  4.6 0.9 copy-done.3
  5.5 67.3 %project_gather.1 = (bf16[32,64,2048]{2,1,0:T(8,128)(2,1)}, bf16[64,2048]{1,0:T(8,128)(2,1)S(1)}, s32[8,8,256]{2,1,0:T(8,128)S(1)}, bf16[8,64,2048]{2,1,0:T(8,128)(2,1)S(1)}) custom-call(bf16[256,512]{1,0:T(8,128)(2,1)S(1)} %bitcast.15, bf16[512,2048]{1,0:T(8,128)(2,1)S(1)} %copy-done.1, bf16[64,2048]{1,0:T(8,128)(2,1)S(1)} %bitcast.16, ...), custom_call_target="tpu_custom_call" | custom-call | tf_op jit(solution)/shard_map/project_gather/pallas_call | solution.py:225
  72.9 0.0 copy-start
  72.9 1.3 copy-done
  74.2 0.7 copy-done.4
  74.9 0.6 copy-done.5
  75.5 0.0 copy-done.9
  75.5 0.7 compare_convert_fusion.cell_expert_ref
  76.3 0.6 pad_add_fusion.where_ref
  76.8 0.0 copy-done.7
  76.9 0.0 copy-done.6
  76.9 0.7 fusion.2.router_ref
  77.6 39.7 %experts.1 = bf16[8,256,2048]{2,1,0:T(8,128)(2,1)} custom-call(s32[2]{0:T(128)} %pad_add_fusion.where_ref, bf16[8,256,2048]{2,1,0:T(8,128)(2,1)} %bitcast.20, s32[8,8,256]{2,1,0:T(8,128)} %copy-done.5, bf16[64,2048]{1,0:T(8,128)(2,1)} %fusion.2.router_ref, bf16[256,64]{1,0:T(8,128)(2,1)} %compare_convert_fusion.cell_expert_ref, ...), custom_call_target="tpu_custom_call" | custom-call | tf_op jit(solution)/shard_map/experts/pallas_call | solution.py:461
  117.3 0.0 copy-done.8
  117.3 0.6 reshape.34.gain
  118.0 63.4 %reduce_norm.1 = (bf16[64,2048]{1,0:T(8,128)(2,1)}, bf16[64,2048]{1,0:T(8,128)(2,1)}) custom-call(bf16[32,64,2048]{2,1,0:T(8,128)(2,1)} %bitcast.17, bf16[64,2048]{1,0:T(8,128)(2,1)} %copy-done.4, bf16[1,2048]{1,0:T(2,128)(2,1)} %reshape.34.gain), custom_call_target="tpu_custom_call" | custom-call | tf_op jit(solution)/shard_map/reduce_norm/pallas_call | solution.py:360
  181.4 1.7 copy.22
  183.1 1.7 copy.23
  (10 shorter events, 0.0 us)
Async XLA Ops:
  0.6 74.9 %copy-start.9 = (s32[60]{0:T(128)S(1)}, s32[60]{0:T(128)}, u32[]{:S(2)}) copy-start(s32[60]{0:T(128)} %param.24) | copy-start | bytes 724
  0.6 76.2 %copy-start.7 = (bf16[2048]{0:T(1024)(128)(2,1)S(1)}, bf16[2048]{0:T(1024)(128)(2,1)}, u32[]{:S(2)}) copy-start(bf16[2048]{0:T(1024)(128)(2,1)} %param.31) | copy-start | bytes 12292
  2.0 1.6 copy-start.1
  3.6 0.9 copy-start.2
  4.6 0.9 copy-start.3
  5.5 71.3 %copy-start.6 = (bf16[2048,60]{0,1:T(8,128)(2,1)S(1)}, bf16[2048,60]{0,1:T(8,128)(2,1)}, u32[]{:S(2)}) copy-start(bf16[2048,60]{0,1:T(8,128)(2,1)} %param.22) | copy-start | bytes 737284
  72.9 1.3 copy-start
  74.2 0.7 copy-start.4
  74.9 0.6 copy-start.5
  77.6 39.7 %copy-start.8 = (bf16[2048]{0:T(1024)(128)(2,1)S(1)}, bf16[2048]{0:T(1024)(128)(2,1)}, u32[]{:S(2)}) copy-start(bf16[2048]{0:T(1024)(128)(2,1)} %param.32) | copy-start | bytes 12292

commit v3 on v2

--- a/solution.py
+++ b/solution.py
@@ -50,13 +50,19 @@
 
 
 def gather_kernel(
-    z_count, tok, attn, w_out, residual, gain, ids, gate_hbm, up_hbm, down_hbm,
+    z_count, tok, attn_hbm, w_out_hbm, residual, gain, ids, gate_hbm, up_hbm, down_hbm,
     rows, hidden, ids_out, shared,
-    outbox, inbox, own, names, gate_w, up_w, down_w, line,
+    attn, w_out, outbox, inbox, own, names, gate_w, up_w, down_w, line,
     ps, pr, zs, zr, fs, fr, ss, sr, cs, cr, local, weight_sem, line_sem,
     izs, izr, ifs, ifr, iss, isr, ics, icr,
 ):
     dp, z, core, first, second, far = place()
+    early = [
+        pltpu.make_async_copy(src, dst, weight_sem.at[3 + i])
+        for i, (src, dst) in enumerate(((w_out_hbm, w_out), (attn_hbm, attn)))
+    ]
+    for load in early:
+        load.start()
     greet(z_count, dp, z, core)
 
     def send(src, dst, s_sem, r_sem, d, e):
@@ -104,6 +110,8 @@
             spot = names.at[core]
             go(send(spot, spot, ics.at[0], icr.at[0], dp, z * 2 + 1 - core))
 
+    for load in early:
+        load.wait()
     for step, k in enumerate((2, 1, 3)):
         q = (dp + k) % N_DP
         outbox[k - 1] = jnp.dot(
@@ -178,8 +186,12 @@
 
     go(over_first(0))
     go(over_second(0, 0))
-    for k in range(1, z_count):
-        go(send(own, block(0, core, dp), zs.at[k], zr.at[k], dp, ((z + k) % z_count) * 2 + core))
+
+    def along_z(k):
+        if k < z_count:
+            go(send(own, block(0, core, dp), zs.at[k], zr.at[k], dp, ((z + k) % z_count) * 2 + core))
+
+    along_z(1)
     go(over_core(0, 0))
 
     def tail(k):
@@ -190,6 +202,7 @@
     for k in range(z_count):
         if k > 0:
             arrived(zr.at[k], block(k, core, dp))
+            along_z(k + 1)
             go(over_first(k))
             go(over_second(k, 0))
             go(over_core(k, 0))
@@ -230,9 +243,12 @@
             jax.ShapeDtypeStruct((z_count * 2, 8, N_DP * tok), jnp.int32),
             jax.ShapeDtypeStruct((z_count * 2, tok, width), bf16),
         ),
-        in_specs=[vmem] * 5 + [pl.BlockSpec(memory_space=pl.ANY)] * 3,
+        in_specs=[pl.BlockSpec(memory_space=pl.ANY)] * 2 + [vmem] * 3
+        + [pl.BlockSpec(memory_space=pl.ANY)] * 3,
         out_specs=(pl.BlockSpec(memory_space=pl.ANY), vmem, vmem, vmem),
         scratch_shapes=[
+            pltpu.VMEM(attn.shape, bf16),
+            pltpu.VMEM(w_out.shape, bf16),
             pltpu.VMEM((N_DP - 1, tok, width), bf16),
             pltpu.VMEM((N_DP - 1, tok, width), bf16),
             pltpu.VMEM((tok, width), bf16),
@@ -246,7 +262,7 @@
             dma((z_count,)), dma((z_count,)),
             dma((2 * z_count,)), dma((2 * z_count,)),
             dma((4 * z_count,)), dma((4 * z_count,)),
-            dma((1,)), dma((3,)), dma((4,)),
+            dma((1,)), dma((5,)), dma((4,)),
             dma((z_count,)), dma((z_count,)),
             dma((1,)), dma((1,)),
             dma((2,)), dma((2,)),
@@ -260,16 +276,34 @@
 
 
 def scatter_kernel(
-    z_count, part, hidden, gain, mixed, final,
-    acc, from_core, from_second, from_first, from_z,
-    cs, cr, ss, sr, fs, fr, zs, zr, local,
+    z_count, tok, results, back, shared, hidden, gain, mixed, final,
+    res_buf, back_buf, shared_buf, whole, outbox, acc, from_core, from_second, from_first, from_z,
+    loads, cs, cr, ss, sr, fs, fr, zs, zr,
 ):
     dp, z, core, first, second, far = place()
+    me = z * 2 + core
+    other = z * 2 + 1 - core
+    pending = []
+    order = sorted(range(1, z_count), key=lambda k: abs(2 * k - z_count)) + [0]
+
+    def level(k):
+        return (z + z_count - k) % z_count
+
+    def arrived(sem, ref):
+        pltpu.make_async_copy(ref, ref, sem).wait()
+
+    def fetches(i):
+        found = []
+        for side in range(2):
+            g = level(order[i]) * 2 + ((1 - core) if side == 0 else core)
+            slot = 2 * (i % 2) + side
+            for n, (src, dst) in enumerate(((results, res_buf), (back, back_buf), (shared, shared_buf))):
+                found.append(pltpu.make_async_copy(src.at[g], dst.at[slot], loads.at[3 * slot + n]))
+        return found
+
+    for fetch in fetches(0):
+        fetch.start()
     greet(z_count, dp, z, core)
-    me = z * 2 + core
-    dest = (dp, first, second, far)
-    pending = []
-    order = list(range(1, z_count)) + [0]
 
     def send(src, dst, s_sem, r_sem, d, e):
         copy = pltpu.make_async_remote_copy(
@@ -277,50 +311,59 @@
             device_id={"dp": d, "ep": e},
         )
         copy.start()
-        pending.append(copy)
-
-    def level(k):
-        return (z + z_count - k) % z_count
-
-    def arrived(sem, ref):
-        pltpu.make_async_copy(ref, ref, sem).wait()
-
-    def begin(k, j):
-        i = 4 * k + j
-        there = (dp, second, first, far)[j]
-        pltpu.make_async_copy(
-            part.at[(level(k) * 2 + core) * N_DP + dest[j]], acc.at[i], local.at[i]
-        ).start()
-        send(
-            part.at[(level(k) * 2 + 1 - core) * N_DP + there], from_core.at[i],
-            cs.at[i], cr.at[i], dp, z * 2 + 1 - core,
-        )
-
-    for j in (3, 2, 1, 0):
-        for k in order:
-            begin(k, j)
+        return copy
+
+    across = {}
+
+    def combine(i, side):
+        k = order[i]
+        slot = 2 * (i % 2) + side
+        dests = (dp, second, first, far) if side == 0 else (dp, first, second, far)
+        for fetch in fetches(i)[3 * side:3 * side + 3]:
+            fetch.wait()
+        whole[...] = jnp.dot(back_buf[slot], res_buf[slot], preferred_element_type=f32).astype(bf16)
+        for j in (3, 2, 1, 0):
+            value = whole[pl.ds(pl.multiple_of(dests[j] * tok, tok), tok), :]
+            if j == 0:
+                value = (value.astype(f32) + shared_buf[slot].astype(f32)).astype(bf16)
+            if side == 1:
+                acc[4 * k + j] = value
+            else:
+                n = 4 * (i % 2) + j
+                if i >= 2:
+                    across[(i - 2, j)].wait_send()
+                outbox[n] = value
+                across[(i, j)] = send(
+                    outbox.at[n], from_core.at[4 * k + j], cs.at[4 * k + j], cr.at[4 * k + j], dp, other
+                )
+
+    def prepare(i):
+        if i + 1 < z_count:
+            for fetch in fetches(i + 1):
+                fetch.start()
+        combine(i, 0)
+        combine(i, 1)
 
     def pair(k, j):
-        i = 4 * k + j
-        arrived(local.at[i], acc.at[i])
-        arrived(cr.at[i], from_core.at[i])
-        return acc[i].astype(f32) + from_core[i].astype(f32)
-
-    for j in (3, 2):
-        for k in order:
+        n = 4 * k + j
+        arrived(cr.at[n], from_core.at[n])
+        return acc[n].astype(f32) + from_core[n].astype(f32)
+
+    def pass_second(k):
+        for j in (3, 2):
             acc[4 * k + j] = pair(k, j).astype(bf16)
-            i = 2 * k + j - 2
-            send(acc.at[4 * k + j], from_second.at[i], ss.at[i], sr.at[i], second, me)
+            n = 2 * k + j - 2
+            pending.append(send(acc.at[4 * k + j], from_second.at[n], ss.at[n], sr.at[n], second, me))
 
     def summed(k, j):
-        i = 2 * k + j
+        n = 2 * k + j
         value = pair(k, j)
-        arrived(sr.at[i], from_second.at[i])
-        return value + from_second[i].astype(f32)
+        arrived(sr.at[n], from_second.at[n])
+        return value + from_second[n].astype(f32)
 
     def pass_first(k):
         acc[4 * k + 1] = summed(k, 1).astype(bf16)
-        send(acc.at[4 * k + 1], from_first.at[k], fs.at[k], fr.at[k], first, me)
+        pending.append(send(acc.at[4 * k + 1], from_first.at[k], fs.at[k], fr.at[k], first, me))
 
     def pass_z(k):
         value = summed(k, 0)
@@ -328,15 +371,21 @@
         value = value + from_first[k].astype(f32)
         if k > 0:
             acc[4 * k] = value.astype(bf16)
-            send(acc.at[4 * k], from_z.at[k], zs.at[k], zr.at[k], dp, level(k) * 2 + core)
-            return None
+            pending.append(
+                send(acc.at[4 * k], from_z.at[k], zs.at[k], zr.at[k], dp, level(k) * 2 + core)
+            )
         return value
 
-    for k in order:
+    prepare(0)
+    for i, k in enumerate(order):
+        pass_second(k)
+        if i + 1 < z_count:
+            prepare(i + 1)
+        if i > 0:
+            pass_z(order[i - 1])
         pass_first(k)
-    for k in order:
-        value = pass_z(k)
-    for k in range(1, z_count):
+    value = pass_z(0)
+    for k in order[:-1]:
         arrived(zr.at[k], from_z.at[k])
         value = value + from_z[k].astype(f32)
     out = (hidden[...].astype(f32) + value).astype(bf16)
@@ -348,33 +397,43 @@
     ).astype(bf16)
     for copy in pending:
         copy.wait_send()
-
-
-def reduce_and_norm(z_count, part, hidden, gain):
+    for i in range(max(0, z_count - 2), z_count):
+        for j in range(4):
+            across[(i, j)].wait_send()
+
+
+def reduce_and_norm(z_count, results, back, shared, hidden, gain):
     tok, width = hidden.shape
+    _, rows, cells = back.shape
     dma = pltpu.SemaphoreType.DMA
     vmem = pl.BlockSpec(memory_space=pltpu.VMEM)
     shape = jax.ShapeDtypeStruct((tok, width), bf16)
-    boxes = [4 * z_count, 4 * z_count, 2 * z_count, z_count, z_count]
-    sems = [4 * z_count] * 2 + [2 * z_count] * 2 + [z_count] * 4 + [4 * z_count]
+    boxes = [8, 4 * z_count, 4 * z_count, 2 * z_count, z_count, z_count]
+    sems = [12] + [4 * z_count] * 2 + [2 * z_count] * 2 + [z_count] * 4
     return pl.pallas_call(
-        functools.partial(scatter_kernel, z_count),
+        functools.partial(scatter_kernel, z_count, tok),
         out_shape=(shape, shape),
-        in_specs=[pl.BlockSpec(memory_space=pl.ANY), vmem, vmem],
+        in_specs=[pl.BlockSpec(memory_space=pl.ANY)] * 3 + [vmem, vmem],
         out_specs=(vmem, vmem),
-        scratch_shapes=[pltpu.VMEM((n, tok, width), bf16) for n in boxes]
+        scratch_shapes=[
+            pltpu.VMEM((4, cells, width), bf16),
+            pltpu.VMEM((4, rows, cells), bf16),
+            pltpu.VMEM((4, tok, width), bf16),
+            pltpu.VMEM((rows, width), bf16),
+        ]
+        + [pltpu.VMEM((n, tok, width), bf16) for n in boxes]
         + [dma((n,)) for n in sems],
         compiler_params=pltpu.CompilerParams(
-            collective_id=1, has_side_effects=True, vmem_limit_bytes=56 << 20
+            collective_id=1, has_side_effects=True, vmem_limit_bytes=60 << 20
         ),
         name="reduce_norm",
-    )(part, hidden, gain)
+    )(results, back, shared, hidden, gain)
 
 
 def expert_kernel(
     groups, experts, tok, where_ref, x_ref, ids_ref, router_ref, cell_expert_ref, cell_number_ref,
     before_ref, source_ref, gate_ref, up_ref, down_ref, shared_ref,
-    out_ref, cells, results, back, logits_ref,
+    results_ref, back_ref, scaled_ref, cells, logits_ref,
 ):
     step = pl.program_id(0)
     wide = N_DP * MOST
@@ -383,7 +442,7 @@
     def _():
         x = x_ref[0]
         logits = rows_dot(x, router_ref[...])
-        logits_ref[step] = logits
+        logits_ref[...] = logits
         lined = logits.T
         numbers = lax.broadcasted_iota(jnp.int32, lined.shape, 0)
         chosen = numbers == ids_ref[0, 0:1, :]
@@ -398,14 +457,18 @@
         spot = jnp.dot(at_cell, rank.astype(bf16), preferred_element_type=f32)
         weight = jnp.dot(at_cell, weights, preferred_element_type=f32)
         here = (named > 0.5) & (spot == cell_number_ref[...])
-        back[step] = jnp.where(here, weight, 0.0).T.astype(bf16)
+        back_ref[0] = jnp.where(here, weight, 0.0).T.astype(bf16)
         picked = jnp.dot(
             jnp.where(here, 1.0, 0.0).astype(bf16), x, preferred_element_type=f32
         ).astype(bf16)
         for e in range(experts):
             cells[e, pl.ds(pl.multiple_of(step * wide, wide), wide), :] = picked[e * wide:(e + 1) * wide]
-
-    @pl.when((step >= groups) & (step < groups + experts))
+        columns = logits_ref[pl.ds(pl.multiple_of(where_ref[0] * tok, tok), tok), :]
+        lane = lax.broadcasted_iota(jnp.int32, columns.shape, 1)
+        score = jnp.sum(jnp.where(lane == where_ref[1], columns, 0.0), axis=1, keepdims=True)
+        scaled_ref[0] = (shared_ref[0].astype(f32) / (1.0 + jnp.exp(-score))).astype(bf16)
+
+    @pl.when(step >= groups)
     def _():
         e = step - groups
         rows = cells[e]
@@ -414,21 +477,7 @@
         hidden = (gate / (1.0 + jnp.exp(-gate)) * up).astype(bf16)
         result = jnp.dot(hidden, down_ref[0], preferred_element_type=f32).astype(bf16)
         for g in range(groups):
-            results[g, pl.ds(pl.multiple_of(e * wide, wide), wide), :] = result[g * wide:(g + 1) * wide]
-
-    @pl.when(step >= groups + experts)
-    def _():
-        g = step - groups - experts
-        out_ref[0] = jnp.dot(back[g], results[g], preferred_element_type=f32).astype(bf16)
-        mine = pl.ds(pl.multiple_of(where_ref[0] * tok, tok), tok)
-        last = where_ref[1]
-        columns = logits_ref[g, mine, :]
-        lane = lax.broadcasted_iota(jnp.int32, columns.shape, 1)
-        score = jnp.sum(jnp.where(lane == last, columns, 0.0), axis=1, keepdims=True)
-        score = 1.0 / (1.0 + jnp.exp(-score))
-        out_ref[0, mine, :] = (
-            out_ref[0, mine, :].astype(f32) + score * shared_ref[0].astype(f32)
-        ).astype(bf16)
+            results_ref[g] = result[g * wide:(g + 1) * wide]
 
 
 def run_experts(x, ids, router, cell_expert, score_row, w_gate, w_up, w_down, shared):
@@ -451,8 +500,8 @@
     def at_expert(i, *_):
         return (jnp.clip(i - groups, 0, experts - 1), 0, 0)
 
-    def at_end(i, *_):
-        return (jnp.clip(i - groups - experts, 0, groups - 1), 0, 0)
+    def at_slice(i, *_):
+        return (0, jnp.clip(i - groups, 0, experts - 1), 0)
 
     def whole(i, *_):
         return (0, 0)
@@ -460,10 +509,14 @@
     where = jnp.stack([lax.axis_index("dp").astype(jnp.int32), jnp.int32(score_row)])
     return pl.pallas_call(
         functools.partial(expert_kernel, groups, experts, tok),
-        out_shape=jax.ShapeDtypeStruct((groups, rows, width), bf16),
+        out_shape=(
+            jax.ShapeDtypeStruct((groups, cells, width), bf16),
+            jax.ShapeDtypeStruct((groups, rows, cells), bf16),
+            jax.ShapeDtypeStruct((groups, tok, width), bf16),
+        ),
         grid_spec=pltpu.PrefetchScalarGridSpec(
             num_scalar_prefetch=1,
-            grid=(2 * groups + experts,),
+            grid=(groups + experts,),
             in_specs=[
                 pl.BlockSpec((1, rows, width), at_group),
                 pl.BlockSpec((1, 8, rows), at_group),
@@ -475,14 +528,16 @@
                 pl.BlockSpec((1, units, width), at_expert),
                 pl.BlockSpec((1, units, width), at_expert),
                 pl.BlockSpec((1, units, width), at_expert),
-                pl.BlockSpec((1, tok, width), at_end),
+                pl.BlockSpec((1, tok, width), at_group),
             ],
-            out_specs=pl.BlockSpec((1, rows, width), at_end),
+            out_specs=(
+                pl.BlockSpec((groups, spread, width), at_slice),
+                pl.BlockSpec((1, rows, cells), at_group),
+                pl.BlockSpec((1, tok, width), at_group),
+            ),
             scratch_shapes=[
                 pltpu.VMEM((experts, groups * spread, width), bf16),
-                pltpu.VMEM((groups, cells, width), bf16),
-                pltpu.VMEM((groups, rows, cells), bf16),
-                pltpu.VMEM((groups, rows, known), f32),
+                pltpu.VMEM((rows, known), f32),
             ],
         ),
         compiler_params=pltpu.CompilerParams(vmem_limit_bytes=56 << 20),
@@ -529,13 +584,12 @@
         z_count, attn_heads[0], w_out, residual[0], gain_post.reshape(1, width), ids,
         w_shared_gate.T, w_shared_up.T, w_shared_down,
     )
-    partial_sums = run_experts(
+    results, back, scaled = run_experts(
         x_all.reshape(groups, rows, width), ids_all, router, cell_expert, expert_count,
         jnp.swapaxes(w_gate, 1, 2), jnp.swapaxes(w_up, 1, 2), w_down, shared,
     )
     mixed_out, final_out = reduce_and_norm(
-        z_count, partial_sums.reshape(groups * N_DP, tok, width), hidden_state,
-        gain_final.reshape(1, width),
+        z_count, results, back, scaled, hidden_state, gain_final.reshape(1, width),
     )
     return (mixed_out[None], final_out[None])
 

time: 185 us -> 162 us (0.88)
  Pallas kernels: 171 us -> 148 us
    pallas_call x1, Pallas kernels: 63.4 us -> 45.5 us  [reduce_and_norm(): pl.pallas_call(functools.partial(scatter_kernel, z_count, tok), out_shape...]
    pallas_call x1, Pallas kernels: 39.7 us -> 34.2 us  [run_experts(): pl.pallas_call(functools.partial(expert_kernel, groups, experts, tok), ou...]
where the time goes in v3:
time: 162 us
  Pallas kernels  148 us (91%)
  local copies, waits for them, and re-layouts  11.5 us (7%)
  other arithmetic  2.12 us (1%)
    pallas_call x1, Pallas kernels, project_and_gather(): pl.pallas_call(functools.partial(gather_kernel, z_count, tok), out_shape=...  68.1 us
    pallas_call x1, Pallas kernels, reduce_and_norm(): pl.pallas_call(functools.partial(scatter_kernel, z_count, tok), out_shape...  45.5 us
    pallas_call x1, Pallas kernels, run_experts(): pl.pallas_call(functools.partial(expert_kernel, groups, experts, tok), ou...  34.2 us
    unnamed x22, local copies, waits for them, and re-layouts  9.49 us

profile of v3, /device:TPU:0, one launch (start us, length us, event | category | flops | bytes accessed | tf_op | source)
XLA Modules:
  0.0 162.0 jit_solution(4524793727219851705)
XLA Ops:
  0.6 0.7 reshape.28.gain
  1.3 0.7 pad.12.ids
  2.0 0.0 copy-start
  2.0 1.6 copy-done
  3.6 0.0 copy-start.2
  3.6 0.9 copy-done.2
  4.6 0.9 copy-done.3
  5.5 68.1 %project_gather.1 = (bf16[32,64,2048]{2,1,0:T(8,128)(2,1)}, bf16[64,2048]{1,0:T(8,128)(2,1)S(1)}, s32[8,8,256]{2,1,0:T(8,128)S(1)}, bf16[8,64,2048]{2,1,0:T(8,128)(2,1)S(1)}) custom-call(bf16[256,512]{1,0:T(8,128)(2,1)S(1)} %bitcast.14, bf16[512,2048]{1,0:T(8,128)(2,1)S(1)} %copy-done, bf16[64,2048]{1,0:T(8,128)(2,1)S(1)} %bitcast.15, ...), custom_call_target="tpu_custom_call" | custom-call | tf_op jit(solution)/shard_map/project_gather/pallas_call | solution.py:238
  73.6 0.0 copy-start.1
  73.6 1.3 copy-done.1
  74.9 0.7 copy-done.4
  75.6 0.6 copy-done.5
  76.2 0.0 copy-done.9
  76.3 0.7 compare_convert_fusion.cell_expert_ref
  77.0 0.7 pad_add_fusion.where_ref
  77.6 0.0 copy-done.7
  77.7 0.0 copy-done.6
  77.7 0.7 fusion.2.router_ref
  78.4 34.2 %experts.1 = (bf16[8,256,2048]{2,1,0:T(8,128)(2,1)}, bf16[8,256,256]{2,1,0:T(8,128)(2,1)}, bf16[8,64,2048]{2,1,0:T(8,128)(2,1)}) custom-call(s32[2]{0:T(128)} %pad_add_fusion.where_ref, bf16[8,256,2048]{2,1,0:T(8,128)(2,1)} %bitcast.18, s32[8,8,256]{2,1,0:T(8,128)} %copy-done.5, bf16[64,2048]{1,0:T(8,128)(2,1)} %fusion.2.router_ref, ...), custom_call_target="tpu_custom_call" | custom-call | tf_op jit(solution)/shard_map/experts/pallas_call | solution.py:510
  112.6 0.0 copy-done.8
  112.6 0.6 reshape.30.gain
  113.2 45.5 %reduce_norm.1 = (bf16[64,2048]{1,0:T(8,128)(2,1)}, bf16[64,2048]{1,0:T(8,128)(2,1)}) custom-call(bf16[8,256,2048]{2,1,0:T(8,128)(2,1)} %get-tuple-element.14.results, bf16[8,256,256]{2,1,0:T(8,128)(2,1)} %get-tuple-element.15.back, bf16[8,64,2048]{2,1,0:T(8,128)(2,1)} %get-tuple-element.16.shared, bf16[64,2048]{1,0:T(8,128)(2,1)} %copy-done.4, ...), custom_call_target="tpu_custom_call" | custom-call | tf_op jit(solution)/shard_map/reduce_norm/pallas_call | solution.py:413
  158.6 1.7 %copy.22 = bf16[1,64,2048]{2,1,0:T(8,128)(2,1)} copy(bf16[1,64,2048]{2,1,0:T(8,128)(2,1)} %bitcast.23) | data formatting | bytes 524288
  160.3 1.7 %copy.23 = bf16[1,64,2048]{2,1,0:T(8,128)(2,1)} copy(bf16[1,64,2048]{2,1,0:T(8,128)(2,1)} %bitcast.22) | data formatting | bytes 524288
  (10 shorter events, 0.0 us)
Async XLA Ops:
  2.0 1.6 copy-start
  3.6 0.9 copy-start.2
  4.6 0.9 copy-start.3
  5.5 70.7 %copy-start.9 = (s32[60]{0:T(128)S(1)}, s32[60]{0:T(128)}, u32[]{:S(2)}) copy-start(s32[60]{0:T(128)} %param.24) | copy-start | bytes 724
  5.5 72.1 %copy-start.7 = (bf16[2048]{0:T(1024)(128)(2,1)S(1)}, bf16[2048]{0:T(1024)(128)(2,1)}, u32[]{:S(2)}) copy-start(bf16[2048]{0:T(1024)(128)(2,1)} %param.31) | copy-start | bytes 12292
  5.5 72.1 %copy-start.6 = (bf16[2048,60]{0,1:T(8,128)(2,1)S(1)}, bf16[2048,60]{0,1:T(8,128)(2,1)}, u32[]{:S(2)}) copy-start(bf16[2048,60]{0,1:T(8,128)(2,1)} %param.22) | copy-start | bytes 737284
  73.6 1.3 copy-start.1
  74.9 0.7 copy-start.4
  75.6 0.6 copy-start.5
  78.4 34.2 %copy-start.8 = (bf16[2048]{0:T(1024)(128)(2,1)S(1)}, bf16[2048]{0:T(1024)(128)(2,1)}, u32[]{:S(2)}) copy-start(bf16[2048]{0:T(1024)(128)(2,1)} %param.32) | copy-start | bytes 12292
